TPU v7x, 128 devices: a whole 4x4x4 slice. The times are simulated.
128 devices in a mesh: bx: 16 (over z, x), by: 8 (over y, core).
Axes of the slice: x: 4, y: 4, z: 4, core: 2. Of those that a mesh axis runs over, the one named last changes fastest.
Arguments:
- weights_re: float32 [1024, 16, 1024], P(None, 'bx', 'by'), may hold values from -3 to 3
- weights_im: float32 [1024, 16, 1024], P(None, 'bx', 'by'), may hold values from -3 to 3
Outputs:
- result_re: float32 [1024, 16, 1024], P(None, 'bx', 'by')
- result_im: float32 [1024, 16, 1024], P(None, 'bx', 'by')
All inputs are finite; a program needn't handle non-finite values.
Results may differ from a plain program's by a relative error of at most 0.0028.
Values sent between devices are 32-bit elements; how exact they have to be, the bound alone decides.
No kernel may reach another device: no remote copies, remote signals or barrier semaphores. Data moves between devices by JAX's collectives and lax.ppermute only.
A program may use at most 64 MiB of HBM per device.

v0:
```python
import jax
import jax.numpy as jnp
from jax import lax
from jax.sharding import PartitionSpec as P

N_FREQ = 16384
CHEB = 8
FX = 32
FY = 32


def swapped(block, axis, apart):
    count = lax.axis_size(axis)
    route = []
    for low in range(count):
        high = low | 1 << apart
        if high != low and high < count:
            route += [(low, high), (high, low)]
    return lax.ppermute(block, axis, route)


def cheb_nodes(cheb_count):
    index_vals = jnp.arange(cheb_count, dtype=jnp.float32)
    node_values = jnp.cos(jnp.pi * (2.0 * index_vals + 1.0) / (2.0 * cheb_count)) / 2.0
    node_high = jnp.floor(node_values * 1024.0) / 1024.0
    node_low = node_values - node_high
    return (node_values, node_high, node_low)


def lagrange_table(cheb_count):
    node_values = cheb_nodes(cheb_count)[0]
    side_offset = jnp.arange(2, dtype=jnp.float32) - 0.5
    child_points = side_offset[:, None] / 2.0 + node_values[None, :] / 2.0
    numerator = child_points[:, :, None, None] - node_values[None, None, None, :]
    diagonal_mask = jnp.eye(cheb_count, dtype=bool)
    denominator = jnp.where(diagonal_mask, 1.0, node_values[:, None] - node_values[None, :])
    factor_table = jnp.where(diagonal_mask[None, None], 1.0, numerator / denominator[None, None])
    lagrange_values = jnp.prod(factor_table, axis=3)
    product_table = jnp.einsum(
        "asi,bzj->abszij", lagrange_values, lagrange_values, precision=lax.Precision.HIGHEST
    )
    return product_table.reshape(2, 2, cheb_count * cheb_count, cheb_count * cheb_count)


def fraction(values):
    return values - jnp.floor(values)


def phase_pair(center_x, center_y, width, freq_x, freq_y, cheb_count):
    node_values, node_high, node_low = cheb_nodes(cheb_count)
    along_x = jnp.repeat(node_values, cheb_count)
    along_y = jnp.tile(node_values, cheb_count)
    high_x = jnp.repeat(node_high, cheb_count)
    high_y = jnp.tile(node_high, cheb_count)
    low_x = jnp.repeat(node_low, cheb_count)
    low_y = jnp.tile(node_low, cheb_count)
    step_x = width * freq_x
    step_y = width * freq_y
    point_x = center_x + width * along_x
    point_y = center_y + width * along_y
    speed_x = (2.0 + jnp.sin(2.0 * jnp.pi * point_x) * jnp.sin(2.0 * jnp.pi * point_y)) / 16.0
    speed_y = (2.0 + jnp.cos(2.0 * jnp.pi * point_x) * jnp.cos(2.0 * jnp.pi * point_y)) / 16.0
    radial = jnp.sqrt((speed_x * freq_x) ** 2 + (speed_y * freq_y) ** 2)
    cycle_total = fraction(center_x * freq_x) + fraction(high_x * step_x) + low_x * step_x
    cycle_total = (
        cycle_total + fraction(center_y * freq_y) + fraction(high_y * step_y) + low_y * step_y
    )
    cycle_total = cycle_total + radial
    phase_angle = 2.0 * jnp.pi * fraction(cycle_total)
    return (jnp.cos(phase_angle), jnp.sin(phase_angle))


def swap_along_x(pair_parts, bit_number):
    return swapped((pair_parts[0], pair_parts[1]), "bx", bit_number)


def swap_along_y(pair_parts, bit_number):
    return swapped((pair_parts[0], pair_parts[1]), "by", bit_number)


def pair_up(mine, theirs, bit_value, stack_axis):
    return tuple(
        (
            jnp.stack(
                [
                    jnp.where(bit_value == 0, mine[member], theirs[member]),
                    jnp.where(bit_value == 0, theirs[member], mine[member]),
                ],
                axis=stack_axis,
            )
            for member in range(2)
        )
    )


def merge_boxes(gathered, parent_x, parent_y, child_width, wave_x, wave_y, cheb_count):
    grid_re, grid_im = gathered
    row_count = wave_y.shape[0]
    group_count = wave_y.shape[1]
    point_count = cheb_count * cheb_count
    side_offset = jnp.arange(2, dtype=jnp.float32) - 0.5
    child_x = parent_x + side_offset * child_width
    child_y = parent_y + side_offset * child_width
    cos_in, sin_in = phase_pair(
        child_x[None, None, :, None, None],
        child_y[None, None, None, :, None],
        child_width,
        wave_x[:, None, None, None, None],
        wave_y[:, :, None, None, None],
        cheb_count,
    )
    mixed_re = grid_re * cos_in - grid_im * sin_in
    mixed_im = grid_re * sin_in + grid_im * cos_in
    interp = lagrange_table(cheb_count).reshape(4 * point_count, point_count)
    identity = jnp.eye(group_count, dtype=jnp.float32)
    interp_block = jnp.einsum("gh,kt->gkht", identity, interp).reshape(
        group_count * 4 * point_count, group_count * point_count
    )
    sum_re = jnp.dot(
        mixed_re.reshape(row_count, -1), interp_block, precision=lax.Precision.HIGHEST
    ).reshape(row_count, group_count, point_count)
    sum_im = jnp.dot(
        mixed_im.reshape(row_count, -1), interp_block, precision=lax.Precision.HIGHEST
    ).reshape(row_count, group_count, point_count)
    cos_out, sin_out = phase_pair(
        parent_x, parent_y, 2.0 * child_width, wave_x[:, None, None], wave_y[:, :, None], cheb_count
    )
    return (sum_re * cos_out + sum_im * sin_out, sum_im * cos_out - sum_re * sin_out)


def on_device(weights_re, weights_im):
    box_count = lax.axis_size("bx")
    level_count = box_count.bit_length() - 1
    cheb_count = CHEB
    point_count = cheb_count * cheb_count
    freq_total = weights_re.shape[0]
    col_index = lax.axis_index("bx")
    row_index = lax.axis_index("by")
    freq_index = jnp.arange(freq_total, dtype=jnp.int32)
    freq_col = (freq_index // FY).astype(jnp.float32)
    freq_row = (freq_index % FY).astype(jnp.float32)
    current = (
        weights_re.reshape(freq_total, 2, point_count),
        weights_im.reshape(freq_total, 2, point_count),
    )
    position_x = jnp.zeros((), jnp.float32)
    position_y = jnp.zeros((2,), jnp.float32)
    for level_index in range(level_count):
        span_size = 2**level_index
        child_width = span_size / box_count
        parent_width = 2.0 * child_width
        col_bit = col_index // span_size % 2
        parent_x = ((col_index // (2 * span_size)).astype(jnp.float32) + 0.5) * parent_width
        parent_y = ((row_index // span_size).astype(jnp.float32) + 0.5) * parent_width
        if level_index == 0:
            received = swap_along_x(current, 0)
            stacked = pair_up(current, received, col_bit, 1)
            gathered = (stacked[0][:, None], stacked[1][:, None])
            bits_y = jnp.arange(2, dtype=jnp.float32)
        else:
            row_bit = row_index // (span_size // 2) % 2
            received = swap_along_x(current, level_index)
            half_set = pair_up(current, received, col_bit, 2)
            received = swap_along_y(half_set, level_index - 1)
            gathered = pair_up(half_set, received, row_bit, 3)
            bits_y = row_bit.astype(jnp.float32) * jnp.ones((2,), jnp.float32)
        position_x = 2.0 * position_x + col_bit.astype(jnp.float32)
        position_y = 2.0 * position_y + bits_y
        wave_x = -N_FREQ / 2.0 + (freq_col * (2 * span_size) + position_x + 0.5) * (
            N_FREQ / (FX * 2 * span_size)
        )
        wave_y = -N_FREQ / 2.0 + (
            freq_row[:, None] * (2 * span_size) + position_y[None, :] + 0.5
        ) * (N_FREQ / (FY * 2 * span_size))
        current = merge_boxes(gathered, parent_x, parent_y, child_width, wave_x, wave_y, cheb_count)
    return (
        current[0].reshape(freq_total, 1, 2 * point_count),
        current[1].reshape(freq_total, 1, 2 * point_count),
    )


def solution(mesh):
    in_specs = (P(None, "bx", "by"), P(None, "bx", "by"))
    out_specs = (P(None, "bx", "by"), P(None, "bx", "by"))
    return jax.shard_map(
        on_device, mesh=mesh, in_specs=in_specs, out_specs=out_specs, check_vma=False
    )
```

profile of v0, /device:TPU:0, one launch (start us, length us, event | category | flops | bytes accessed | tf_op | source)
XLA Modules:
  0.0 250.4 jit_solution(9289285098589805733)
XLA Ops:
  16.9 10.0 %collective-permute-done.1 = f32[1024,2,64]{0,2,1:T(8,128)} collective-permute-done((f32[1024,2,64]{0,2,1:T(8,128)S(1)}, f32[1024,2,64]{0,2,1:T(8,128)}, u32[]{:S(2)}, u32[]{:S(2)}) %collective-permute-start.1) | collective-permute-done | bytes 524320 | tf_op jit(solution)/shard_map/ppermute | solution.py:19
  28.3 9.5 %multiply_add_fusion.3 = (f32[1024,2,2,2,64]{0,4,1,2,3:T(8,128)S(1)}, f32[1024,2,2,2,64]{0,4,1,2,3:T(8,128)S(1)}) fusion(f32[1024,2]{0,1:T(2,128)S(1)} %get-tuple-element.84, f32[2,2,64]{2,0,1:T(2,128)S(1)} %get-tuple-element.128, f32[1024,2,2,64]{0,3,1,2:T(8,128)S(1)} %multiply_multiply_fusion.3, f32[1024,2,64]{0,2,1:T(8,128)S(1)} %get-tuple-element.61, ...), kind=kLoop, calls=%fused_computation.20 | loop fusion | flops 8650752 | bytes 8938496 | tf_op jit(solution)/shard_map/add | solution.py:113
  39.6 3.5 %multiply_add_fusion.7 = (f32[1024,2,64]{0,2,1:T(8,128)S(1)}, f32[1024,2,64]{0,2,1:T(8,128)S(1)}) fusion(f32[1024,2,64]{0,2,1:T(8,128)S(1)} %fusion.109, f32[1024,2]{0,1:T(2,128)S(1)} %get-tuple-element.84, f32[64]{0:T(128)S(1)} %get-tuple-element.121, f32[1024,64]{0,1:T(8,128)S(1)} %multiply_multiply_fusion.7, f32[1024,2]{0,1:T(2,128)S(1)} %get-tuple-element.83, ...), kind=kOutput, calls=%fused_computation.105 | convolution fusion | flops 807927808 | bytes 4481792 | tf_op jit(solution)/shard_map/dot_general | solution.py:122
  43.1 3.4 %collective-permute-start.2 = (f32[1024,2,64]{0,2,1:T(8,128)S(1)}, f32[1024,2,64]{0,2,1:T(8,128)S(1)}, u32[]{:S(2)}, u32[]{:S(2)}) collective-permute-start(f32[1024,2,64]{0,2,1:T(8,128)S(1)} %get-tuple-element.34), channel_id=1, source_target_pairs={{0,16},{16,0},{8,24},{24,8},{32,48},{48,32},{40,56},{56,40},{64,80... | collective-permute-start | bytes 1572872 | tf_op jit(solution)/shard_map/ppermute | solution.py:19
  47.5 12.0 %collective-permute-done.2 = f32[1024,2,64]{0,2,1:T(8,128)S(1)} collective-permute-done((f32[1024,2,64]{0,2,1:T(8,128)S(1)}, f32[1024,2,64]{0,2,1:T(8,128)S(1)}, u32[]{:S(2)}, u32[]{:S(2)}) %collective-permute-start.2) | collective-permute-done | bytes 524320 | tf_op jit(solution)/shard_map/ppermute | solution.py:19
  60.6 8.1 %collective-permute-done.4 = f32[1024,2,64]{0,2,1:T(8,128)S(1)} collective-permute-done((f32[1024,2,64]{0,2,1:T(8,128)S(1)}, f32[1024,2,64]{0,2,1:T(8,128)S(1)}, u32[]{:S(2)}, u32[]{:S(2)}) %collective-permute-start.4) | collective-permute-done | bytes 524320 | tf_op jit(solution)/shard_map/ppermute | solution.py:19
  75.8 9.1 %multiply_add_fusion.2 = (f32[1024,2,2,2,64]{0,4,1,2,3:T(8,128)S(1)}, f32[1024,2,2,2,64]{0,4,1,2,3:T(8,128)S(1)}) fusion(f32[1024,2,2,1,64]{0,4,1,2,3:T(8,128)S(1)} %get-tuple-element.29, f32[1024,2,2,1,64]{0,4,1,2,3:T(8,128)S(1)} %get-tuple-element.28, f32[1024,2,2,1,64]{0,4,1,2,3:T(8,128)S(1)} %get-tuple-element.27, ...), kind=kLoop, calls=%fused_computation.18 | loop fusion | flops 9437184 | bytes 11035648 | tf_op jit(solution)/shard_map/add | solution.py:113
  87.4 3.5 %multiply_add_fusion.6 = (f32[1024,2,64]{0,2,1:T(8,128)S(1)}, f32[1024,2,64]{0,2,1:T(8,128)S(1)}) fusion(f32[1024,2,64]{0,2,1:T(8,128)S(1)} %fusion.110, f32[1024,2]{0,1:T(2,128)S(1)} %get-tuple-element.72, f32[64]{0:T(128)S(1)} %copy-done.15, f32[1024,64]{0,1:T(8,128)S(1)} %multiply_multiply_fusion.6, f32[1024,2]{0,1:T(2,128)S(1)} %get-tuple-element.71, ...), kind=kOutput, calls=%fused_computation.98 | convolution fusion | flops 807927808 | bytes 4481792 | tf_op jit(solution)/shard_map/dot_general | solution.py:122
  90.9 2.2 collective-permute-start.6
  93.6 12.3 %collective-permute-done.6 = f32[1024,2,64]{0,2,1:T(8,128)S(1)} collective-permute-done((f32[1024,2,64]{0,2,1:T(8,128)S(1)}, f32[1024,2,64]{0,2,1:T(8,128)S(1)}, u32[]{:S(2)}, u32[]{:S(2)}) %collective-permute-start.6) | collective-permute-done | bytes 524320 | tf_op jit(solution)/shard_map/ppermute | solution.py:19
  108.7 8.2 %collective-permute-done.8 = f32[1024,2,64]{0,2,1:T(8,128)S(1)} collective-permute-done((f32[1024,2,64]{0,2,1:T(8,128)S(1)}, f32[1024,2,64]{0,2,1:T(8,128)S(1)}, u32[]{:S(2)}, u32[]{:S(2)}) %collective-permute-start.8) | collective-permute-done | bytes 524320 | tf_op jit(solution)/shard_map/ppermute | solution.py:19
  121.2 12.2 %collective-permute-done.7 = f32[1024,2,2,64]{0,3,1,2:T(8,128)} collective-permute-done((f32[1024,2,2,64]{0,3,1,2:T(8,128)}, f32[1024,2,2,64]{0,3,1,2:T(8,128)}, u32[]{:S(2)}, u32[]{:S(2)}) %collective-permute-start.7) | collective-permute-done | bytes 1048608 | tf_op jit(solution)/shard_map/ppermute | solution.py:19
  134.9 19.7 %collective-permute-done.9 = f32[1024,2,2,64]{0,3,1,2:T(8,128)S(1)} collective-permute-done((f32[1024,2,2,64]{0,3,1,2:T(8,128)}, f32[1024,2,2,64]{0,3,1,2:T(8,128)S(1)}, u32[]{:S(2)}, u32[]{:S(2)}) %collective-permute-start.9) | collective-permute-done | bytes 1048608 | tf_op jit(solution)/shard_map/ppermute | solution.py:19
  154.8 9.1 %multiply_add_fusion.1 = (f32[1024,2,2,2,64]{0,4,1,2,3:T(8,128)S(1)}, f32[1024,2,2,2,64]{0,4,1,2,3:T(8,128)S(1)}) fusion(f32[1024,2,2,1,64]{0,4,1,2,3:T(8,128)S(1)} %get-tuple-element.25, f32[1024,2,2,1,64]{0,4,1,2,3:T(8,128)S(1)} %get-tuple-element.24, f32[1024,2,2,1,64]{0,4,1,2,3:T(8,128)S(1)} %get-tuple-element.23, ...), kind=kLoop, calls=%fused_computation.16 | loop fusion | flops 9437184 | bytes 11035648 | tf_op jit(solution)/shard_map/add | solution.py:113
  166.4 3.5 %multiply_add_fusion.5 = (f32[1024,2,64]{0,2,1:T(8,128)S(1)}, f32[1024,2,64]{0,2,1:T(8,128)S(1)}) fusion(f32[1024,2,64]{0,2,1:T(8,128)S(1)} %fusion.111, f32[1024,2]{0,1:T(2,128)S(1)} %get-tuple-element.68, f32[64]{0:T(128)S(1)} %get-tuple-element.109, f32[1024,64]{0,1:T(8,128)S(1)} %multiply_multiply_fusion.5, f32[1024,2]{0,1:T(2,128)S(1)} %get-tuple-element.66, ...), kind=kOutput, calls=%fused_computation.91 | convolution fusion | flops 807927808 | bytes 4481792 | tf_op jit(solution)/shard_map/dot_general | solution.py:122
  169.9 3.5 %collective-permute-start.10 = (f32[1024,2,64]{0,2,1:T(8,128)S(1)}, f32[1024,2,64]{0,2,1:T(8,128)S(1)}, u32[]{:S(2)}, u32[]{:S(2)}) collective-permute-start(f32[1024,2,64]{0,2,1:T(8,128)S(1)} %get-tuple-element.30), channel_id=1, source_target_pairs={{0,64},{64,0},{8,72},{72,8},{16,80},{80,16},{24,88},{88,24},{32,96... | collective-permute-start | bytes 1572872 | tf_op jit(solution)/shard_map/ppermute | solution.py:19
  173.7 12.6 %collective-permute-done.10 = f32[1024,2,64]{0,2,1:T(8,128)S(1)} collective-permute-done((f32[1024,2,64]{0,2,1:T(8,128)S(1)}, f32[1024,2,64]{0,2,1:T(8,128)S(1)}, u32[]{:S(2)}, u32[]{:S(2)}) %collective-permute-start.10) | collective-permute-done | bytes 524320 | tf_op jit(solution)/shard_map/ppermute | solution.py:19
  187.5 3.1 %collective-permute-start.11 = (f32[1024,2,2,64]{0,3,1,2:T(8,128)}, f32[1024,2,2,64]{0,3,1,2:T(8,128)}, u32[]{:S(2)}, u32[]{:S(2)}) collective-permute-start(f32[1024,2,2,64]{0,3,1,2:T(8,128)} %pad_maximum_fusion.12), channel_id=1, source_target_pairs={{0,4},{4,0},{1,5},{5,1},{2,6},{6,2},{3,7},{7,3},{8,12},{12,8},{9,1... | collective-permute-start | bytes 3145736 | tf_op jit(solution)/shard_map/ppermute | solution.py:19
  190.6 4.9 %collective-permute-done.12 = f32[1024,2,64]{0,2,1:T(8,128)S(1)} collective-permute-done((f32[1024,2,64]{0,2,1:T(8,128)S(1)}, f32[1024,2,64]{0,2,1:T(8,128)S(1)}, u32[]{:S(2)}, u32[]{:S(2)}) %collective-permute-start.12) | collective-permute-done | bytes 524320 | tf_op jit(solution)/shard_map/ppermute | solution.py:19
  196.6 3.1 %collective-permute-start.13 = (f32[1024,2,2,64]{0,3,1,2:T(8,128)}, f32[1024,2,2,64]{0,3,1,2:T(8,128)S(1)}, u32[]{:S(2)}, u32[]{:S(2)}) collective-permute-start(f32[1024,2,2,64]{0,3,1,2:T(8,128)} %pad_maximum_fusion.13), channel_id=1, source_target_pairs={{0,4},{4,0},{1,5},{5,1},{2,6},{6,2},{3,7},{7,3},{8,12},{12,8},{9,1... | collective-permute-start | bytes 3145736 | tf_op jit(solution)/shard_map/ppermute | solution.py:19
  201.2 14.1 %collective-permute-done.11 = f32[1024,2,2,64]{0,3,1,2:T(8,128)} collective-permute-done((f32[1024,2,2,64]{0,3,1,2:T(8,128)}, f32[1024,2,2,64]{0,3,1,2:T(8,128)}, u32[]{:S(2)}, u32[]{:S(2)}) %collective-permute-start.11) | collective-permute-done | bytes 1048608 | tf_op jit(solution)/shard_map/ppermute | solution.py:19
  216.8 15.9 %collective-permute-done.13 = f32[1024,2,2,64]{0,3,1,2:T(8,128)S(1)} collective-permute-done((f32[1024,2,2,64]{0,3,1,2:T(8,128)}, f32[1024,2,2,64]{0,3,1,2:T(8,128)S(1)}, u32[]{:S(2)}, u32[]{:S(2)}) %collective-permute-start.13) | collective-permute-done | bytes 1048608 | tf_op jit(solution)/shard_map/ppermute | solution.py:19
  232.9 9.1 %multiply_subtract_fusion = (f32[1024,2,2,2,64]{0,4,1,2,3:T(8,128)S(1)}, f32[1024,2,2,2,64]{0,4,1,2,3:T(8,128)S(1)}) fusion(f32[1024,2,2,1,64]{0,4,1,2,3:T(8,128)S(1)} %get-tuple-element.21, f32[1024,2,2,1,64]{0,4,1,2,3:T(8,128)S(1)} %get-tuple-element.20, f32[1024,2,2,1,64]{0,4,1,2,3:T(8,128)S(1)} %get-tuple-element.19, ...), kind=kLoop, calls=%fused_computation.15 | loop fusion | flops 9437184 | bytes 11035648 | tf_op jit(solution)/shard_map/sub | solution.py:112
  244.6 3.5 %multiply_subtract_fusion.4 = (f32[1024,2,64]{0,2,1:T(8,128)S(1)}, f32[1024,2,64]{0,2,1:T(8,128)S(1)}) fusion(f32[1024,2,64]{0,2,1:T(8,128)S(1)} %fusion.112, f32[64]{0:T(128)S(1)} %reshape.3025, f32[1024,64]{0,1:T(8,128)S(1)} %copy-done.6, f32[1024,2]{0,1:T(2,128)S(1)} %get-tuple-element.64, f32[1024,2]{0,1:T(2,128)S(1)} %get-tuple-element.62, ...), kind=kOutput, calls=%fused_computation.83 | convolution fusion | flops 807927808 | bytes 4473600 | tf_op jit(solution)/shard_map/dot_general | solution.py:119
  (195 shorter events, 52.8 us)
Async XLA Ops:
  1.9 15.0 %collective-permute-start = (f32[1024,2,64]{0,2,1:T(8,128)S(1)}, f32[1024,2,64]{0,2,1:T(8,128)}, u32[]{:S(2)}, u32[]{:S(2)}) collective-permute-start(f32[1024,2,64]{0,2,1:T(8,128)S(1)} %bitcast.132), channel_id=1, source_target_pairs={{0,8},{8,0},{16,24},{24,16},{32,40},{40,32},{48,56},{56,48},{64,72... | collective-permute-start | bytes 1572872 | tf_op jit(solution)/shard_map/ppermute | solution.py:19
  4.8 22.0 %collective-permute-start.1 = (f32[1024,2,64]{0,2,1:T(8,128)S(1)}, f32[1024,2,64]{0,2,1:T(8,128)}, u32[]{:S(2)}, u32[]{:S(2)}) collective-permute-start(f32[1024,2,64]{0,2,1:T(8,128)S(1)} %bitcast.134), channel_id=1, source_target_pairs={{0,8},{8,0},{16,24},{24,16},{32,40},{40,32},{48,56},{56,48},{64,72... | collective-permute-start | bytes 1572872 | tf_op jit(solution)/shard_map/ppermute | solution.py:19
  11.3 2.3 copy-start.10
  39.6 7.3 %copy-start.11 = (f32[64]{0:T(128)S(1)}, f32[64]{0:T(128)}, u32[]{:S(2)}) copy-start(f32[64]{0:T(128)} %copy-done.10) | copy-start | bytes 772
  43.1 16.4 %collective-permute-start.2 = (f32[1024,2,64]{0,2,1:T(8,128)S(1)}, f32[1024,2,64]{0,2,1:T(8,128)S(1)}, u32[]{:S(2)}, u32[]{:S(2)}) collective-permute-start(f32[1024,2,64]{0,2,1:T(8,128)S(1)} %get-tuple-element.34), channel_id=1, source_target_pairs={{0,16},{16,0},{8,24},{24,8},{32,48},{48,32},{40,56},{56,40},{64,80... | collective-permute-start | bytes 1572872 | tf_op jit(solution)/shard_map/ppermute | solution.py:19
  46.5 22.2 %collective-permute-start.4 = (f32[1024,2,64]{0,2,1:T(8,128)S(1)}, f32[1024,2,64]{0,2,1:T(8,128)S(1)}, u32[]{:S(2)}, u32[]{:S(2)}) collective-permute-start(f32[1024,2,64]{0,2,1:T(8,128)S(1)} %get-tuple-element.35), channel_id=1, source_target_pairs={{0,16},{16,0},{8,24},{24,8},{32,48},{48,32},{40,56},{56,40},{64,80... | collective-permute-start | bytes 1572872 | tf_op jit(solution)/shard_map/ppermute | solution.py:19
  60.6 12.5 %collective-permute-start.3 = (f32[1024,2,2,64]{0,3,1,2:T(8,128)}, f32[1024,2,2,64]{0,3,1,2:T(8,128)}, u32[]{:S(2)}, u32[]{:S(2)}) collective-permute-start(f32[1024,2,2,64]{0,3,1,2:T(8,128)} %pad_maximum_fusion.8), channel_id=1, source_target_pairs={{0,1},{1,0},{2,3},{3,2},{4,5},{5,4},{6,7},{7,6},{8,9},{9,8},{10,11... | collective-permute-start | bytes 3145736 | tf_op jit(solution)/shard_map/ppermute | solution.py:19
  69.9 4.7 %collective-permute-start.5 = (f32[1024,2,2,64]{0,3,1,2:T(8,128)}, f32[1024,2,2,64]{0,3,1,2:T(8,128)S(1)}, u32[]{:S(2)}, u32[]{:S(2)}) collective-permute-start(f32[1024,2,2,64]{0,3,1,2:T(8,128)} %pad_maximum_fusion.9), channel_id=1, source_target_pairs={{0,1},{1,0},{2,3},{3,2},{4,5},{5,4},{6,7},{7,6},{8,9},{9,8},{10,11... | collective-permute-start | bytes 3145736 | tf_op jit(solution)/shard_map/ppermute | solution.py:19
  87.4 5.7 %copy-start.14 = (f32[2]{0:T(128)S(1)}, f32[2]{0:T(128)}, u32[]{:S(2)}) copy-start(f32[2]{0:T(128)} %broadcast_add_fusion.2) | copy-start | bytes 28
  87.4 5.9 %copy-start.13 = (f32[2]{0:T(128)S(1)}, f32[2]{0:T(128)}, u32[]{:S(2)}) copy-start(f32[2]{0:T(128)} %copy-done.12) | copy-start | bytes 28
  90.9 15.0 %collective-permute-start.6 = (f32[1024,2,64]{0,2,1:T(8,128)S(1)}, f32[1024,2,64]{0,2,1:T(8,128)S(1)}, u32[]{:S(2)}, u32[]{:S(2)}) collective-permute-start(f32[1024,2,64]{0,2,1:T(8,128)S(1)} %get-tuple-element.32), channel_id=1, source_target_pairs={{0,32},{32,0},{8,40},{40,8},{16,48},{48,16},{24,56},{56,24},{64,96... | collective-permute-start | bytes 1572872 | tf_op jit(solution)/shard_map/ppermute | solution.py:19
  93.4 23.5 %collective-permute-start.8 = (f32[1024,2,64]{0,2,1:T(8,128)S(1)}, f32[1024,2,64]{0,2,1:T(8,128)S(1)}, u32[]{:S(2)}, u32[]{:S(2)}) collective-permute-start(f32[1024,2,64]{0,2,1:T(8,128)S(1)} %get-tuple-element.33), channel_id=1, source_target_pairs={{0,32},{32,0},{8,40},{40,8},{16,48},{48,16},{24,56},{56,24},{64,96... | collective-permute-start | bytes 1572872 | tf_op jit(solution)/shard_map/ppermute | solution.py:19
  107.1 26.3 %collective-permute-start.7 = (f32[1024,2,2,64]{0,3,1,2:T(8,128)}, f32[1024,2,2,64]{0,3,1,2:T(8,128)}, u32[]{:S(2)}, u32[]{:S(2)}) collective-permute-start(f32[1024,2,2,64]{0,3,1,2:T(8,128)} %pad_maximum_fusion.10), channel_id=1, source_target_pairs={{0,2},{2,0},{1,3},{3,1},{4,6},{6,4},{5,7},{7,5},{8,10},{10,8},{9,1... | collective-permute-start | bytes 3145736 | tf_op jit(solution)/shard_map/ppermute | solution.py:19
  118.1 36.4 %collective-permute-start.9 = (f32[1024,2,2,64]{0,3,1,2:T(8,128)}, f32[1024,2,2,64]{0,3,1,2:T(8,128)S(1)}, u32[]{:S(2)}, u32[]{:S(2)}) collective-permute-start(f32[1024,2,2,64]{0,3,1,2:T(8,128)} %pad_maximum_fusion.11), channel_id=1, source_target_pairs={{0,2},{2,0},{1,3},{3,1},{4,6},{6,4},{5,7},{7,5},{8,10},{10,8},{9,1... | collective-permute-start | bytes 3145736 | tf_op jit(solution)/shard_map/ppermute | solution.py:19
  134.8 19.9 %copy-start.2 = (f32[1024,2,64]{0,2,1:T(8,128)S(1)}, f32[1024,2,64]{0,2,1:T(8,128)}, u32[]{:S(2)}) copy-start(f32[1024,2,64]{0,2,1:T(8,128)} %get-tuple-element.100) | copy-start | bytes 1572868
  134.8 19.9 %copy-start.3 = (f32[1024,2,64]{0,2,1:T(8,128)S(1)}, f32[1024,2,64]{0,2,1:T(8,128)}, u32[]{:S(2)}) copy-start(f32[1024,2,64]{0,2,1:T(8,128)} %get-tuple-element.101) | copy-start | bytes 1572868
  169.9 16.4 %collective-permute-start.10 = (f32[1024,2,64]{0,2,1:T(8,128)S(1)}, f32[1024,2,64]{0,2,1:T(8,128)S(1)}, u32[]{:S(2)}, u32[]{:S(2)}) collective-permute-start(f32[1024,2,64]{0,2,1:T(8,128)S(1)} %get-tuple-element.30), channel_id=1, source_target_pairs={{0,64},{64,0},{8,72},{72,8},{16,80},{80,16},{24,88},{88,24},{32,96... | collective-permute-start | bytes 1572872 | tf_op jit(solution)/shard_map/ppermute | solution.py:19
  173.6 21.8 %collective-permute-start.12 = (f32[1024,2,64]{0,2,1:T(8,128)S(1)}, f32[1024,2,64]{0,2,1:T(8,128)S(1)}, u32[]{:S(2)}, u32[]{:S(2)}) collective-permute-start(f32[1024,2,64]{0,2,1:T(8,128)S(1)} %get-tuple-element.31), channel_id=1, source_target_pairs={{0,64},{64,0},{8,72},{72,8},{16,80},{80,16},{24,88},{88,24},{32,96... | collective-permute-start | bytes 1572872 | tf_op jit(solution)/shard_map/ppermute | solution.py:19
  187.5 12.2 %copy-start.16 = (f32[8]{0:T(128)S(1)}, f32[8]{0:T(128)}, u32[]{:S(2)}) copy-start(f32[8]{0:T(128)} %get-tuple-element.143) | copy-start | bytes 100
  187.5 12.2 %copy-start.17 = (f32[8]{0:T(128)S(1)}, f32[8]{0:T(128)}, u32[]{:S(2)}) copy-start(f32[8]{0:T(128)} %get-tuple-element.134) | copy-start | bytes 100
  187.5 27.9 %collective-permute-start.11 = (f32[1024,2,2,64]{0,3,1,2:T(8,128)}, f32[1024,2,2,64]{0,3,1,2:T(8,128)}, u32[]{:S(2)}, u32[]{:S(2)}) collective-permute-start(f32[1024,2,2,64]{0,3,1,2:T(8,128)} %pad_maximum_fusion.12), channel_id=1, source_target_pairs={{0,4},{4,0},{1,5},{5,1},{2,6},{6,2},{3,7},{7,3},{8,12},{12,8},{9,1... | collective-permute-start | bytes 3145736 | tf_op jit(solution)/shard_map/ppermute | solution.py:19
  196.6 36.0 %collective-permute-start.13 = (f32[1024,2,2,64]{0,3,1,2:T(8,128)}, f32[1024,2,2,64]{0,3,1,2:T(8,128)S(1)}, u32[]{:S(2)}, u32[]{:S(2)}) collective-permute-start(f32[1024,2,2,64]{0,3,1,2:T(8,128)} %pad_maximum_fusion.13), channel_id=1, source_target_pairs={{0,4},{4,0},{1,5},{5,1},{2,6},{6,2},{3,7},{7,3},{8,12},{12,8},{9,1... | collective-permute-start | bytes 3145736 | tf_op jit(solution)/shard_map/ppermute | solution.py:19
  216.7 16.1 %copy-start = (f32[1024,2,64]{0,2,1:T(8,128)S(1)}, f32[1024,2,64]{0,2,1:T(8,128)}, u32[]{:S(2)}) copy-start(f32[1024,2,64]{0,2,1:T(8,128)} %get-tuple-element.98) | copy-start | bytes 1572868
  216.8 16.1 %copy-start.1 = (f32[1024,2,64]{0,2,1:T(8,128)S(1)}, f32[1024,2,64]{0,2,1:T(8,128)}, u32[]{:S(2)}) copy-start(f32[1024,2,64]{0,2,1:T(8,128)} %get-tuple-element.99) | copy-start | bytes 1572868
  (8 other events, 9.1 us)
where the time goes:
time: 255 us; the launch traced here: 250 us
  waiting for transfers between devices  131 us (51%)
  other arithmetic  64.7 us (25%)
  starting transfers between devices  21.9 us (9%)
  matrix products  19.1 us (7%)
  local copies, waits for them, and re-layouts  11.8 us (5%)
    ppermute x14, waiting for transfers between devices, swapped(): return lax.ppermute(block, axis, route)  131 us
    add x3, other arithmetic, merge_boxes(): mixed_im = grid_re * sin_in + grid_im * cos_in  27.7 us
    ppermute x14, starting transfers between devices, swapped(): return lax.ppermute(block, axis, route)  21.9 us
    another operation x20, other arithmetic, pair_up(): jnp.stack([jnp.where(bit_value == 0, mine[member], theirs[member]), jnp.w...  13.5 us
    dot_general x4, matrix products, merge_boxes(): jnp.dot(mixed_im.reshape(row_count, -1), interp_block, precision=lax.Prec...  11.7 us
    sub x1, other arithmetic, merge_boxes(): mixed_re = grid_re * cos_in - grid_im * sin_in  9.12 us
    unnamed x41, local copies, waits for them, and re-layouts  7.69 us
    dot_general x4, matrix products, merge_boxes(): jnp.dot(mixed_re.reshape(row_count, -1), interp_block, precision=lax.Prec...  7.35 us
  transfers between devices with their start and end apart: 14, of which 12 were waited for; matrix products, arithmetic and copies ran while one was open for 12% of the time, Pallas kernels for 0%

commit v1 on v0

v1 whole, which is shorter than its diff:
```python
import jax
import jax.numpy as jnp
import numpy as np
from jax import lax
from jax.experimental import pallas as pl
from jax.experimental.pallas import tpu as pltpu
from jax.sharding import PartitionSpec as P

N_FREQ = 16384
CHEB = 8
FX = 32
FY = 32
BOXES = 16
LEVELS = 4
POINTS = CHEB * CHEB
LANES = 2 * POINTS
ROWS = 8


def _fit(function, count):
    grid = np.cos(np.pi * (np.arange(count) + 0.5) / count) * 0.125 + 0.125
    return [float(c) for c in np.polyfit(grid, function(np.sqrt(grid)), count - 1)]


SIN_TERMS = _fit(lambda u: 2.0 * np.sin(np.pi * u) / u, 6)
COS_TERMS = _fit(lambda u: np.cos(np.pi * u), 6)


def horner(terms, value):
    total = terms[0] * value + terms[1]
    for term in terms[2:]:
        total = total * value + term
    return total


def turn(cycles):
    rest = cycles - jnp.round(cycles)
    square = rest * rest
    twice_sin = rest * horner(SIN_TERMS, square)
    half_cos = horner(COS_TERMS, square)
    return 1.0 - 0.5 * (twice_sin * twice_sin), twice_sin * half_cos


def nodes():
    value = (np.cos(np.pi * (2.0 * np.arange(CHEB) + 1.0) / (2.0 * CHEB)) / 2.0).astype(np.float32)
    high = (np.floor(value * np.float32(1024.0)) / np.float32(1024.0)).astype(np.float32)
    return value, high, value - high


def node_rows():
    value, high, low = nodes()
    lane = np.arange(LANES)
    first, second = lane // CHEB % CHEB, lane % CHEB
    rows = [value[first], value[second], high[first], low[first], high[second], low[second], lane // POINTS]
    rows.append(np.zeros(LANES))
    return np.stack(rows).astype(np.float32)


def lagrange_table():
    value = jnp.asarray(nodes()[0])
    side = jnp.arange(2, dtype=jnp.float32) - 0.5
    child = side[:, None] / 2.0 + value[None, :] / 2.0
    numerator = child[:, :, None, None] - value[None, None, None, :]
    diagonal = jnp.eye(CHEB, dtype=bool)
    denominator = jnp.where(diagonal, 1.0, value[:, None] - value[None, :])
    factor = jnp.where(diagonal[None, None], 1.0, numerator / denominator[None, None])
    return jnp.prod(factor, axis=3)


def interp_blocks():
    table = lagrange_table()
    interp = jnp.einsum("asi,bzj->abszij", table, table, precision=lax.Precision.HIGHEST)
    interp = interp.reshape(2, 2 * POINTS, POINTS)
    zero = jnp.zeros_like(interp)
    block = jnp.concatenate(
        [jnp.concatenate([interp, zero], axis=2), jnp.concatenate([zero, interp], axis=2)], axis=1
    )
    high = lax.reduce_precision(block, 8, 7)
    low = block - high
    return jnp.concatenate([high, low], axis=2).astype(jnp.bfloat16)


def path_offset(level, path):
    return sum((2 * (path >> bit & 1) - 1) * (N_FREQ // FX / 4) / 2**bit for bit in range(level))


def path_base(level):
    return 2**level - 1


def boxes_at(level):
    return BOXES >> level


def point_base(level):
    return sum((boxes_at(at) // 2) ** 2 for at in range(level))


def table_kernel(owner_ref, node_ref, t0c, t0s, t1c, t1s, t2c, t2s, t3c, t3s, fc, fs, sq1, sq2, sqp, pp, qq, lin):
    shape = (ROWS, LANES)
    row = lambda index: jnp.broadcast_to(node_ref[index : index + 1, :], shape)
    owner = owner_ref[0]
    fx = (owner // (FY // ROWS)).astype(jnp.float32)
    fy0 = (owner % (FY // ROWS) * ROWS).astype(jnp.float32)
    width = N_FREQ / FX
    sub = lax.broadcasted_iota(jnp.int32, shape, 0).astype(jnp.float32)
    k1 = jnp.full(shape, -N_FREQ / 2.0 + (fx + 0.5) * width, jnp.float32)
    k2 = -N_FREQ / 2.0 + (fy0 + sub + 0.5) * width
    for level in range(LEVELS + 1):
        for path in range(2**level):
            off = path_offset(level, path)
            sq1[path_base(level) + path] = (k1 + off) * (k1 + off)
            sq2[path_base(level) + path] = (k2 + off) * (k2 + off)
    upper = row(6) > 0.5
    for level in range(LEVELS + 1):
        n = boxes_at(level)
        w = 1.0 / n
        across, down = max(n // 2, 1), max(n // 2, 1)
        part_x = [turn((sx + 0.5) * w + w * row(0)) for sx in range(across)]
        part_y = []
        for pair in range(down):
            center = (2 * pair + row(6) + 0.5) * w if level < LEVELS else 0.5
            part_y.append(turn(center + w * row(1)))
        for sx in range(across):
            for pair in range(down):
                c1 = (2.0 + part_x[sx][1] * part_y[pair][1]) / 16.0
                c2 = (2.0 + part_x[sx][0] * part_y[pair][0]) / 16.0
                at = point_base(level) + sx * down + pair
                pp[at] = c1 * c1
                qq[at] = c2 * c2

    def frac(v):
        return v - jnp.floor(v)

    w = 1.0 / BOXES
    for jx in range(2):
        for jy in range(2):
            s1 = w * (k1 + path_offset(1, jx))
            s2 = w * (k2 + path_offset(1, jy))
            along = frac(row(2) * s1) + row(3) * s1 + frac(row(4) * s2) + row(5) * s2
            lin[2 * jx + jy] = along
            lin[4 + 2 * jx + jy] = (N_FREQ / FX / 4) / BOXES * ((2 * jx - 1) * row(0) + (2 * jy - 1) * row(1))

    @pl.loop(0, 8)
    def _(sx):
        for pair in range(8):
            p, q = pp[sx * 8 + pair], qq[sx * 8 + pair]
            for jx in range(2):
                for jy in range(2):
                    r = jnp.sqrt(p * sq1[1 + jx] + q * sq2[1 + jy])
                    c, s = turn(r - jnp.round(r) + lin[2 * jx + jy])
                    at = (2 * jx + jy) * 64 + sx * 8 + pair
                    t0c[at] = c
                    t0s[at] = s

    def level_of(level, ax, ay, sx, pair, out_c, out_s):
        n = boxes_at(level)
        half, span = n // 2, 2**level
        point = point_base(level) + sx * half + pair
        p, q = pp[point], qq[point]
        base = path_base(level)
        r0 = jnp.sqrt(p * sq1[base + ax] + q * sq2[base + ay])
        nxt = path_base(level + 1)
        for jx in range(2):
            for jy in range(2):
                j = 2 * jx + jy
                r = jnp.sqrt(p * sq1[nxt + ax + jx * span] + q * sq2[nxt + ay + jy * span])
                c, s = turn((r - r0) + lin[4 + j])
                path = j * span * span + ax * span + ay
                if level < 3:
                    at = (path * half + sx) * half + pair
                    out_c[at] = c
                    out_s[at] = s
                else:
                    out_c[2 * path] = c
                    out_s[2 * path] = s
                    out_c[2 * path + 1] = pltpu.roll(c, POINTS, 1)
                    out_s[2 * path + 1] = pltpu.roll(s, POINTS, 1)

    @pl.loop(0, 16)
    def _(step):
        a, sx = step // 4, step % 4
        for pair in range(4):
            level_of(1, a // 2, a % 2, sx, pair, t1c, t1s)

    @pl.loop(0, 16)
    def _(a):
        for sx in range(2):
            for pair in range(2):
                level_of(2, a // 4, a % 4, sx, pair, t2c, t2s)

    @pl.loop(0, 16)
    def _(step):
        for a in range(4):
            level_of(3, step // 2, step % 2 * 4 + a, 0, 0, t3c, t3s)

    base = path_base(LEVELS)
    for pair in range(8):
        off = jnp.where(upper, path_offset(LEVELS, 2 * pair + 1), path_offset(LEVELS, 2 * pair))
        k = k2 + off
        sqp[pair] = k * k
        lin[8 + pair] = frac(row(4) * k) + row(5) * k
    for path in range(16):
        k = k1 + path_offset(LEVELS, path)
        lin[16 + path] = frac(row(2) * k) + row(3) * k

    @pl.loop(0, 16)
    def _(ax):
        p, q = pp[point_base(LEVELS)], qq[point_base(LEVELS)]
        for pair in range(8):
            r = jnp.sqrt(p * sq1[base + ax] + q * sqp[pair])
            c, s = turn(r - jnp.round(r) + lin[16 + ax] + lin[8 + pair])
            fc[ax * 8 + pair] = c
            fs[ax * 8 + pair] = s


def merge_kernel(data_ref, w_ref, t0c, t0s, t1c, t1s, t2c, t2s, t3c, t3s, fc, fs, out_ref, ar, ai, br, bi, lhs):
    tables = ((t0c, t0s), (t1c, t1s), (t2c, t2s), (t3c, t3s))
    buffers = (None, (ar, ai), (br, bi), (ar, ai))

    for level in range(LEVELS):
        n = boxes_at(level)
        half, span = n // 2, 2**level
        cos_ref, sin_ref = tables[level]

        def load(index, level=level):
            if level == 0:
                return data_ref[index, 0:ROWS], data_ref[index, ROWS : 2 * ROWS]
            return buffers[level][0][index], buffers[level][1][index]

        def source(q, cx, e, level=level, n=n, half=half):
            if level == 3:
                index = (2 * q + e) * 2 + cx
                return index, index
            quarter = n // 4
            m, pair = q // quarter, 2 * (q % quarter) + e
            a, sx = m // half, 2 * (m % half) + cx
            index = (a * n + sx) * half + pair
            if sx >= half:
                sx, pair = sx - half, (pair + quarter) % half
            return index, (a * half + sx) * half + pair

        count = half * half * span * span if level < 3 else 2 * span * span

        @pl.loop(0, 4)
        def _(j, level=level, n=n, half=half, span=span, load=load, source=source, count=count,
              cos_ref=cos_ref, sin_ref=sin_ref):
            jx, jy = j // 2, j % 2
            for part in range(2):
                for cx in range(2):
                    for e in range(2):
                        for i in range(0, 16, 2):
                            pieces = []
                            for q in (16 * part + i, 16 * part + i + 1):
                                index, factor = source(q, cx, e)
                                xr, xi = load(index)
                                c, s = cos_ref[j * count + factor], sin_ref[j * count + factor]
                                pieces.append((xr * c - xi * s, xr * s + xi * c))
                            for which in range(2):
                                value = jnp.concatenate([pieces[0][which], pieces[1][which]], axis=0)
                                high = value.astype(jnp.bfloat16)
                                low = (value - high.astype(jnp.float32)).astype(jnp.bfloat16)
                                at = 128 * which + 8 * i
                                lhs[cx, pl.ds(at, 16), LANES * e : LANES * (e + 1)] = high
                                lhs[cx, pl.ds(256 + at, 16), LANES * e : LANES * (e + 1)] = low
                total = jnp.dot(lhs[0], w_ref[0], preferred_element_type=jnp.float32)
                total = total + jnp.dot(lhs[1], w_ref[1], preferred_element_type=jnp.float32)
                both = total[0:256, 0:LANES] + total[0:256, LANES:] + total[256:512, 0:LANES]
                for i in range(16):
                    q = 16 * part + i
                    re, im = both[8 * i : 8 * i + 8], both[128 + 8 * i : 128 + 8 * i + 8]
                    if level < 3:
                        block = n * n // 8
                        a, rest = q // block, q % block
                        ax, ay = a // span, a % span
                        at = ((jx * span + ax) * 2 * span + jy * span + ay) * block + rest
                        nr, ni = buffers[level + 1]
                        nr[at] = re
                        ni[at] = im
                    else:
                        ax, pair = q // 4, q % 4
                        at = (jx * 8 + ax) * 8 + jy * 4 + pair
                        c, s = fc[at], fs[at]
                        out_ref[at, 0:ROWS] = re * c + im * s
                        out_ref[at, ROWS : 2 * ROWS] = im * c - re * s


def tables(owner):
    f32 = jnp.float32
    vreg = (ROWS, LANES)
    sizes = (256, 256, 256, 512, 128)
    full = pl.BlockSpec(memory_space=pltpu.VMEM)
    return pl.pallas_call(
        table_kernel,
        out_shape=[jax.ShapeDtypeStruct((size,) + vreg, f32) for size in sizes for _ in range(2)],
        in_specs=[pl.BlockSpec(memory_space=pltpu.SMEM), full],
        out_specs=[full] * 10,
        scratch_shapes=[
            pltpu.VMEM((31,) + vreg, f32),
            pltpu.VMEM((31,) + vreg, f32),
            pltpu.VMEM((8,) + vreg, f32),
            pltpu.VMEM((88,) + vreg, f32),
            pltpu.VMEM((88,) + vreg, f32),
            pltpu.VMEM((32,) + vreg, f32),
        ],
        cost_estimate=pl.CostEstimate(flops=40_000_000, bytes_accessed=11 << 20, transcendentals=1_400_000),
        compiler_params=pltpu.CompilerParams(vmem_limit_bytes=20 << 20),
        name="phase_tables",
    )(owner, jnp.asarray(node_rows()))


def merge(data, weights, factors):
    f32 = jnp.float32
    vreg = (ROWS, LANES)
    full = pl.BlockSpec(memory_space=pltpu.VMEM)
    return pl.pallas_call(
        merge_kernel,
        out_shape=jax.ShapeDtypeStruct((128, 2 * ROWS, LANES), f32),
        in_specs=[full] * 12,
        out_specs=full,
        scratch_shapes=[pltpu.VMEM((128,) + vreg, f32)] * 4 + [pltpu.VMEM((2, 512, 256), jnp.bfloat16)],
        cost_estimate=pl.CostEstimate(flops=2_000_000_000, bytes_accessed=13 << 20, transcendentals=0),
        compiler_params=pltpu.CompilerParams(vmem_limit_bytes=32 << 20),
        name="merge_levels",
    )(data, weights, *factors)


def on_device(weights_re, weights_im):
    devices = 128
    owner = lax.axis_index("bx") * lax.axis_size("by") + lax.axis_index("by")
    sent = jnp.concatenate(
        [weights_re.reshape(devices, ROWS, LANES), weights_im.reshape(devices, ROWS, LANES)], axis=1
    )
    data = lax.all_to_all(sent, ("bx", "by"), 0, 0, tiled=True)
    factors = tables(owner.astype(jnp.int32).reshape(1))
    result = merge(data, interp_blocks(), factors)
    back = lax.all_to_all(result, ("bx", "by"), 0, 0, tiled=True)
    shape = (devices * ROWS, 1, LANES)
    return back[:, :ROWS].reshape(shape), back[:, ROWS:].reshape(shape)


def solution(mesh):
    specs = (P(None, "bx", "by"), P(None, "bx", "by"))
    return jax.shard_map(on_device, mesh=mesh, in_specs=specs, out_specs=specs, check_vma=False)
```

time: 255 us -> 84.5 us (0.33); the launches traced: 250 us -> 83.8 us
  waiting for transfers between devices: 131 us -> 0.01 us
  other arithmetic: 64.7 us -> 3.13 us
  blocking collectives: 0 us -> 28.6 us
  matrix products: 19.1 us -> 0 us
  Pallas kernels: 0 us -> 18.3 us
  starting transfers between devices: 21.9 us -> 11.2 us
  local copies, waits for them, and re-layouts: 11.8 us -> 21.8 us
    ppermute x14 -> x0, waiting for transfers between devices: 131 us -> none  [swapped(): return lax.ppermute(block, axis, route)]
    add x19 -> x1, other arithmetic: 31.7 us -> 0.07 us  [lagrange_table(): child = side[:, None] / 2.0 + value[None, :] / 2.0]
    all_to_all x0 -> x1, blocking collectives: none -> 28.6 us  [on_device(): back = lax.all_to_all(result, ('bx', 'by'), 0, 0, tiled=True)]
    ppermute x14 -> x0, starting transfers between devices: 21.9 us -> none  [swapped(): return lax.ppermute(block, axis, route)]
    dot_general x8 -> x0, matrix products: 19.1 us -> none  [the longest x4 11.7 us: merge_boxes(): jnp.dot(mixed_im.reshape(row_count, -1), interp_block, precision=lax.Prec...]
    pallas_call x0 -> x2, Pallas kernels: none -> 18.3 us  [the longest x1 9.51 us: merge(): pl.pallas_call(merge_kernel, out_shape=jax.ShapeDtypeStruct((128, 2 * ROW...]
    sub x21 -> x1, other arithmetic: 13.8 us -> 0.07 us  [lagrange_table(): numerator = child[:, :, None, None] - value[None, None, None, :]]
    another operation x21 -> x1, other arithmetic: 13.5 us -> 0.11 us  [the longest x20 13.5 us: pair_up(): jnp.stack([jnp.where(bit_value == 0, mine[member], theirs[member]), jnp.w...]
  transfers between devices with their start and end apart: 14 -> 1, of which waited for: 12 -> 0; matrix products, arithmetic and copies ran while one was open for 12% -> 2% of each run, Pallas kernels for 0% -> 11%
where the time goes in v1:
time: 84.5 us; the launch traced here: 83.8 us
  blocking collectives  28.6 us (34%)
  local copies, waits for them, and re-layouts  21.8 us (26%)
  Pallas kernels  18.3 us (22%)
  starting transfers between devices  11.2 us (13%)
  other arithmetic  3.13 us (4%)
    all_to_all x1, blocking collectives, on_device(): back = lax.all_to_all(result, ('bx', 'by'), 0, 0, tiled=True)  28.6 us
    unnamed x44, local copies, waits for them, and re-layouts  20 us
    all_to_all x1, starting transfers between devices, on_device(): data = lax.all_to_all(sent, ('bx', 'by'), 0, 0, tiled=True)  11.2 us
    pallas_call x1, Pallas kernels, merge(): pl.pallas_call(merge_kernel, out_shape=jax.ShapeDtypeStruct((128, 2 * ROW...  9.51 us
    pallas_call x1, Pallas kernels, tables(): pl.pallas_call(table_kernel, out_shape=[jax.ShapeDtypeStruct((size,) + vr...  8.83 us
    concatenate x1, other arithmetic, on_device(): jnp.concatenate([weights_re.reshape(devices, ROWS, LANES), weights_im.res...  2.27 us
  transfers between devices with their start and end apart: 1, of which 0 were waited for; matrix products, arithmetic and copies ran while one was open for 2% of the time, Pallas kernels for 11%

profile of v1, /device:TPU:0, one launch (start us, length us, event | category | flops | bytes accessed | tf_op | source)
XLA Modules:
  0.0 83.8 jit_solution(17852075099000410146)
XLA Ops:
  0.7 2.3 %pad_maximum_fusion = f32[128,16,128]{2,1,0:T(8,128)} fusion(f32[128,8,128]{2,1,0:T(8,128)} %bitcast.15, f32[128,8,128]{2,1,0:T(8,128)} %bitcast.16), kind=kLoop, calls=%fused_computation | loop fusion | flops 262144 | bytes 2097152 | tf_op jit(solution)/shard_map/concatenate | solution.py:331
  2.9 11.2 %all-to-all-start = ((f32[128,16,128]{2,1,0:T(8,128)}), f32[128,16,128]{2,1,0:T(8,128)S(1)}, u32[]{:S(2)}, u32[]{:S(2)}) async-start(f32[128,16,128]{2,1,0:T(8,128)} %pad_maximum_fusion), calls=%async_computation | async-start | bytes 2097152 | tf_op jit(solution)/shard_map/all_to_all | solution.py:334
  15.7 8.8 %phase_tables.1 = (f32[256,8,128]{2,1,0:T(8,128)S(1)}, f32[256,8,128]{2,1,0:T(8,128)S(1)}, f32[256,8,128]{2,1,0:T(8,128)S(1)}, f32[256,8,128]{2,1,0:T(8,128)S(1)...) custom-call(s32[1]{0:T(128)} %bitcast.3.owner_ref, ...), custom_call_target="tpu_custom_call" | custom-call | flops 40000000 | bytes 11534336 | tf_op jit(solution)/shard_map/phase_tables/pallas_call | solution.py:293
  24.5 1.3 %copy-done = f32[512,8,128]{2,1,0:T(8,128)} copy-done((f32[512,8,128]{2,1,0:T(8,128)}, f32[512,8,128]{2,1,0:T(8,128)S(1)}, u32[]{:S(2)}) %copy-start) | copy-done | bytes 2097176
  25.8 1.0 %copy-done.2 = f32[256,8,128]{2,1,0:T(8,128)} copy-done((f32[256,8,128]{2,1,0:T(8,128)}, f32[256,8,128]{2,1,0:T(8,128)S(1)}, u32[]{:S(2)}) %copy-start.2) | copy-done | bytes 1048600
  26.8 1.0 %copy-done.4 = f32[256,8,128]{2,1,0:T(8,128)} copy-done((f32[256,8,128]{2,1,0:T(8,128)}, f32[256,8,128]{2,1,0:T(8,128)S(1)}, u32[]{:S(2)}) %copy-start.4) | copy-done | bytes 1048600
  27.8 1.0 %copy-done.6 = f32[256,8,128]{2,1,0:T(8,128)} copy-done((f32[256,8,128]{2,1,0:T(8,128)}, f32[256,8,128]{2,1,0:T(8,128)S(1)}, u32[]{:S(2)}) %copy-start.6) | copy-done | bytes 1048600
  28.8 1.0 %copy-done.8 = f32[256,8,128]{2,1,0:T(8,128)} copy-done((f32[256,8,128]{2,1,0:T(8,128)}, f32[256,8,128]{2,1,0:T(8,128)S(1)}, u32[]{:S(2)}) %copy-start.8) | copy-done | bytes 1048600
  29.8 1.1 %copy-done.10 = f32[256,8,128]{2,1,0:T(8,128)} copy-done((f32[256,8,128]{2,1,0:T(8,128)}, f32[256,8,128]{2,1,0:T(8,128)S(1)}, u32[]{:S(2)}) %copy-start.10) | copy-done | bytes 1048600
  30.8 1.0 %copy-done.12 = f32[256,8,128]{2,1,0:T(8,128)} copy-done((f32[256,8,128]{2,1,0:T(8,128)}, f32[256,8,128]{2,1,0:T(8,128)S(1)}, u32[]{:S(2)}) %copy-start.12) | copy-done | bytes 1048600
  31.9 0.8 copy-done.14
  32.7 0.8 copy-done.16
  33.6 1.6 %copy-done.1 = f32[512,8,128]{2,1,0:T(8,128)S(1)} copy-done((f32[512,8,128]{2,1,0:T(8,128)S(1)}, f32[512,8,128]{2,1,0:T(8,128)}, u32[]{:S(2)}) %copy-start.1) | copy-done | bytes 2097176
  35.2 1.2 %copy-done.3 = f32[256,8,128]{2,1,0:T(8,128)S(1)} copy-done((f32[256,8,128]{2,1,0:T(8,128)S(1)}, f32[256,8,128]{2,1,0:T(8,128)}, u32[]{:S(2)}) %copy-start.3) | copy-done | bytes 1048600
  36.4 1.2 %copy-done.5 = f32[256,8,128]{2,1,0:T(8,128)S(1)} copy-done((f32[256,8,128]{2,1,0:T(8,128)S(1)}, f32[256,8,128]{2,1,0:T(8,128)}, u32[]{:S(2)}) %copy-start.5) | copy-done | bytes 1048600
  37.7 1.2 %copy-done.7 = f32[256,8,128]{2,1,0:T(8,128)S(1)} copy-done((f32[256,8,128]{2,1,0:T(8,128)S(1)}, f32[256,8,128]{2,1,0:T(8,128)}, u32[]{:S(2)}) %copy-start.7) | copy-done | bytes 1048600
  38.9 1.2 %copy-done.9 = f32[256,8,128]{2,1,0:T(8,128)S(1)} copy-done((f32[256,8,128]{2,1,0:T(8,128)S(1)}, f32[256,8,128]{2,1,0:T(8,128)}, u32[]{:S(2)}) %copy-start.9) | copy-done | bytes 1048600
  40.1 1.2 %copy-done.11 = f32[256,8,128]{2,1,0:T(8,128)S(1)} copy-done((f32[256,8,128]{2,1,0:T(8,128)S(1)}, f32[256,8,128]{2,1,0:T(8,128)}, u32[]{:S(2)}) %copy-start.11) | copy-done | bytes 1048600
  41.3 1.2 %copy-done.13 = f32[256,8,128]{2,1,0:T(8,128)S(1)} copy-done((f32[256,8,128]{2,1,0:T(8,128)S(1)}, f32[256,8,128]{2,1,0:T(8,128)}, u32[]{:S(2)}) %copy-start.13) | copy-done | bytes 1048600
  42.6 1.0 %copy-done.15 = f32[128,8,128]{2,1,0:T(8,128)S(1)} copy-done((f32[128,8,128]{2,1,0:T(8,128)S(1)}, f32[128,8,128]{2,1,0:T(8,128)}, u32[]{:S(2)}) %copy-start.15) | copy-done | bytes 524312
  43.6 1.0 %copy-done.17 = f32[128,8,128]{2,1,0:T(8,128)S(1)} copy-done((f32[128,8,128]{2,1,0:T(8,128)S(1)}, f32[128,8,128]{2,1,0:T(8,128)}, u32[]{:S(2)}) %copy-start.17) | copy-done | bytes 524312
  44.7 9.5 %merge_levels.1 = f32[128,16,128]{2,1,0:T(8,128)S(1)} custom-call(f32[128,16,128]{2,1,0:T(8,128)S(1)} %all-to-all-done.data_ref, bf16[2,256,256]{2,1,0:T(8,128)(2,1)S(1)} %pad_maximum_fusion.1.w_ref, f32[256,8,128]{2,1,0:T(8,128)S(1)} %copy-done.3, f32[256,8,128]{2,1,0:T(8,128)S(1)} %copy-done.5, f32[256,8,128]{2,1,0:T(8,128)S(1)} %copy-done.7, ...), custom_call_target="tpu_custom_call" | custom-call | flops 2000000000 | bytes 13631488 | tf_op jit(solution)/shard_map/merge_levels/pallas_call | solution.py:316
  54.2 28.6 %all_to_all.10 = f32[128,16,128]{2,1,0:T(8,128)S(1)} all-to-all(f32[128,16,128]{2,1,0:T(8,128)S(1)} %merge_levels.1), channel_id=1, replica_groups=mesh['bx'=16,'by'=8] {'bx','by'}, dimensions={0} | all-to-all | bytes 2097152 | tf_op jit(solution)/shard_map/all_to_all | solution.py:337
  82.8 1.0 %fusion.2 = (f32[128,8,128]{2,1,0:T(8,128)}, f32[128,8,128]{2,1,0:T(8,128)}) fusion(f32[128,16,128]{2,1,0:T(8,128)S(1)} %all_to_all.10), kind=kLoop, calls=%fused_computation.16 | loop fusion | bytes 2097152 | tf_op jit(solution)/shard_map/slice | solution.py:339
  (40 shorter events, 1.7 us)
Async XLA Ops:
  0.6 13.5 %copy-start.19 = (f32[8]{0:T(128)S(1)}, f32[8]{0:T(128)}, u32[]{:S(2)}) copy-start(f32[8]{0:T(128)} %constant.36) | copy-start | bytes 100
  0.6 13.5 %copy-start.20 = (f32[8]{0:T(128)S(1)}, f32[8]{0:T(128)}, u32[]{:S(2)}) copy-start(f32[8]{0:T(128)} %constant.28.clone) | copy-start | bytes 100
  0.7 13.6 %copy-start.21 = (f32[8]{0:T(128)S(1)}, f32[8]{0:T(128)}, u32[]{:S(2)}) copy-start(f32[8]{0:T(128)} %constant.35) | copy-start | bytes 100
  2.9 12.7 %copy-start.18 = (f32[8,128]{1,0:T(8,128)S(1)}, f32[8,128]{1,0:T(8,128)}, u32[]{:S(2)}) copy-start(f32[8,128]{1,0:T(8,128)} %constant.27.clone.node_ref) | copy-start | bytes 12292
  2.9 30.7 %all-to-all-start = ((f32[128,16,128]{2,1,0:T(8,128)}), f32[128,16,128]{2,1,0:T(8,128)S(1)}, u32[]{:S(2)}, u32[]{:S(2)}) async-start(f32[128,16,128]{2,1,0:T(8,128)} %pad_maximum_fusion), calls=%async_computation | async-start | bytes 2097152 | tf_op jit(solution)/shard_map/all_to_all | solution.py:334
  24.5 1.3 %copy-start = (f32[512,8,128]{2,1,0:T(8,128)}, f32[512,8,128]{2,1,0:T(8,128)S(1)}, u32[]{:S(2)}) copy-start(f32[512,8,128]{2,1,0:T(8,128)S(1)} %get-tuple-element.19.t3s) | copy-start | bytes 6291460
  25.8 1.0 %copy-start.2 = (f32[256,8,128]{2,1,0:T(8,128)}, f32[256,8,128]{2,1,0:T(8,128)S(1)}, u32[]{:S(2)}) copy-start(f32[256,8,128]{2,1,0:T(8,128)S(1)} %get-tuple-element.12.t0c) | copy-start | bytes 3145732
  26.8 1.0 %copy-start.4 = (f32[256,8,128]{2,1,0:T(8,128)}, f32[256,8,128]{2,1,0:T(8,128)S(1)}, u32[]{:S(2)}) copy-start(f32[256,8,128]{2,1,0:T(8,128)S(1)} %get-tuple-element.13.t0s) | copy-start | bytes 3145732
  27.8 1.0 %copy-start.6 = (f32[256,8,128]{2,1,0:T(8,128)}, f32[256,8,128]{2,1,0:T(8,128)S(1)}, u32[]{:S(2)}) copy-start(f32[256,8,128]{2,1,0:T(8,128)S(1)} %get-tuple-element.14.t1c) | copy-start | bytes 3145732
  28.8 1.0 %copy-start.8 = (f32[256,8,128]{2,1,0:T(8,128)}, f32[256,8,128]{2,1,0:T(8,128)S(1)}, u32[]{:S(2)}) copy-start(f32[256,8,128]{2,1,0:T(8,128)S(1)} %get-tuple-element.15.t1s) | copy-start | bytes 3145732
  29.8 1.1 %copy-start.10 = (f32[256,8,128]{2,1,0:T(8,128)}, f32[256,8,128]{2,1,0:T(8,128)S(1)}, u32[]{:S(2)}) copy-start(f32[256,8,128]{2,1,0:T(8,128)S(1)} %get-tuple-element.16.t2c) | copy-start | bytes 3145732
  30.8 1.0 %copy-start.12 = (f32[256,8,128]{2,1,0:T(8,128)}, f32[256,8,128]{2,1,0:T(8,128)S(1)}, u32[]{:S(2)}) copy-start(f32[256,8,128]{2,1,0:T(8,128)S(1)} %get-tuple-element.17.t2s) | copy-start | bytes 3145732
  31.9 0.8 copy-start.14
  32.7 0.8 copy-start.16
  33.6 1.6 %copy-start.1 = (f32[512,8,128]{2,1,0:T(8,128)S(1)}, f32[512,8,128]{2,1,0:T(8,128)}, u32[]{:S(2)}) copy-start(f32[512,8,128]{2,1,0:T(8,128)} %copy-done) | copy-start | bytes 6291460
  35.2 1.2 %copy-start.3 = (f32[256,8,128]{2,1,0:T(8,128)S(1)}, f32[256,8,128]{2,1,0:T(8,128)}, u32[]{:S(2)}) copy-start(f32[256,8,128]{2,1,0:T(8,128)} %copy-done.2) | copy-start | bytes 3145732
  36.4 1.2 %copy-start.5 = (f32[256,8,128]{2,1,0:T(8,128)S(1)}, f32[256,8,128]{2,1,0:T(8,128)}, u32[]{:S(2)}) copy-start(f32[256,8,128]{2,1,0:T(8,128)} %copy-done.4) | copy-start | bytes 3145732
  37.7 1.2 %copy-start.7 = (f32[256,8,128]{2,1,0:T(8,128)S(1)}, f32[256,8,128]{2,1,0:T(8,128)}, u32[]{:S(2)}) copy-start(f32[256,8,128]{2,1,0:T(8,128)} %copy-done.6) | copy-start | bytes 3145732
  38.9 1.2 %copy-start.9 = (f32[256,8,128]{2,1,0:T(8,128)S(1)}, f32[256,8,128]{2,1,0:T(8,128)}, u32[]{:S(2)}) copy-start(f32[256,8,128]{2,1,0:T(8,128)} %copy-done.8) | copy-start | bytes 3145732
  40.1 1.2 %copy-start.11 = (f32[256,8,128]{2,1,0:T(8,128)S(1)}, f32[256,8,128]{2,1,0:T(8,128)}, u32[]{:S(2)}) copy-start(f32[256,8,128]{2,1,0:T(8,128)} %copy-done.10) | copy-start | bytes 3145732
  41.3 1.2 %copy-start.13 = (f32[256,8,128]{2,1,0:T(8,128)S(1)}, f32[256,8,128]{2,1,0:T(8,128)}, u32[]{:S(2)}) copy-start(f32[256,8,128]{2,1,0:T(8,128)} %copy-done.12) | copy-start | bytes 3145732
  42.6 1.0 %copy-start.15 = (f32[128,8,128]{2,1,0:T(8,128)S(1)}, f32[128,8,128]{2,1,0:T(8,128)}, u32[]{:S(2)}) copy-start(f32[128,8,128]{2,1,0:T(8,128)} %copy-done.14) | copy-start | bytes 1572868
  43.6 1.0 %copy-start.17 = (f32[128,8,128]{2,1,0:T(8,128)S(1)}, f32[128,8,128]{2,1,0:T(8,128)}, u32[]{:S(2)}) copy-start(f32[128,8,128]{2,1,0:T(8,128)} %copy-done.16) | copy-start | bytes 1572868

commit v2 on v1

v2 whole, which is shorter than its diff:
```python
import jax
import jax.numpy as jnp
import numpy as np
from jax import lax
from jax.experimental import pallas as pl
from jax.experimental.pallas import tpu as pltpu
from jax.sharding import PartitionSpec as P

N_FREQ = 16384
CHEB = 8
FX = 32
FY = 32
BOXES = 16
LEVELS = 4
POINTS = CHEB * CHEB
LANES = 2 * POINTS
ROWS = 8


def _fit(function, count):
    grid = np.cos(np.pi * (np.arange(count) + 0.5) / count) * 0.125 + 0.125
    return [float(c) for c in np.polyfit(grid, function(np.sqrt(grid)), count - 1)]


SIN_TERMS = _fit(lambda u: 2.0 * np.sin(np.pi * u) / u, 6)
COS_TERMS = _fit(lambda u: np.cos(np.pi * u), 6)


def horner(terms, value):
    total = terms[0] * value + terms[1]
    for term in terms[2:]:
        total = total * value + term
    return total


def turn(cycles):
    rest = cycles - jnp.round(cycles)
    square = rest * rest
    twice_sin = rest * horner(SIN_TERMS, square)
    half_cos = horner(COS_TERMS, square)
    return 1.0 - 0.5 * (twice_sin * twice_sin), twice_sin * half_cos


def nodes():
    value = (np.cos(np.pi * (2.0 * np.arange(CHEB) + 1.0) / (2.0 * CHEB)) / 2.0).astype(np.float32)
    high = (np.floor(value * np.float32(1024.0)) / np.float32(1024.0)).astype(np.float32)
    return value, high, value - high


def node_rows():
    value, high, low = nodes()
    lane = np.arange(LANES)
    first, second = lane // CHEB % CHEB, lane % CHEB
    rows = [value[first], value[second], high[first], low[first], high[second], low[second], lane // POINTS]
    rows.append(np.zeros(LANES))
    return np.stack(rows).astype(np.float32)


def path_offset(level, path):
    return sum((2 * (path >> bit & 1) - 1) * (N_FREQ // FX / 4) / 2**bit for bit in range(level))


def path_base(level):
    return 2**level - 1


def boxes_at(level):
    return BOXES >> level


def point_base(level):
    return sum((boxes_at(at) // 2) ** 2 for at in range(level))


TABLE_BASE = (0, 0, 256, 512, 1024)
TABLE_SIZE = 1152
TABLE_PARTS = ((0, 256), (256, 256), (512, 512), (1024, 128))


def interp_rows(node_ref, w_ref):
    shape = (LANES, LANES)
    source = lax.broadcasted_iota(jnp.int32, shape, 0)
    target = lax.broadcasted_iota(jnp.int32, shape, 1)
    value = nodes()[0]

    def pick(index):
        return sum(jnp.where(index == i, float(value[i]), 0.0) for i in range(CHEB))

    def lagrange(point, index):
        z = pick(index)
        total = None
        for j in range(CHEB):
            other = index != j
            factor = jnp.where(other, (point - float(value[j])) / jnp.where(other, z - float(value[j]), 1.0), 1.0)
            total = factor if total is None else total * factor
        return total

    first, second = source // CHEB % CHEB, source % CHEB
    row, column = target // CHEB % CHEB, target % CHEB
    cy = (source // POINTS).astype(jnp.float32)
    along_y = lagrange((cy - 0.5) / 2.0 + pick(second) / 2.0, column)
    for cx in range(2):
        block = lagrange((cx - 0.5) / 2.0 + pick(first) / 2.0, row) * along_y
        for pair in range(2):
            inside = target // POINTS == pair
            mine = jnp.where(inside, block, 0.0)
            high = mine.astype(jnp.bfloat16)
            low = (mine - high.astype(jnp.float32)).astype(jnp.bfloat16)
            at = (2 * cx + pair) * LANES
            w_ref[at : at + LANES, 0:LANES] = high
            w_ref[at : at + LANES, LANES : 2 * LANES] = low


def part_copies(make, part):
    at, size = TABLE_PARTS[part]
    return [make(which, pl.ds(at, size), 2 * part + which) for which in range(2)]


def table_kernel(owner_ref, node_ref, w_ref, cos0_ref, sin0_ref, rest_ref, sq1, sq2, sqp, pp, qq, lin, cos_ref, sin_ref, sems):
    def send(which, rows, sem):
        held = (cos_ref, sin_ref)[which]
        return pltpu.make_async_copy(held.at[rows], rest_ref.at[which, rows], sems.at[sem])

    def flush(part):
        for copy in part_copies(send, part):
            copy.start()

    shape = (ROWS, LANES)
    row = lambda index: jnp.broadcast_to(node_ref[index : index + 1, :], shape)
    owner = owner_ref[0]
    fx = (owner // (FY // ROWS)).astype(jnp.float32)
    fy0 = (owner % (FY // ROWS) * ROWS).astype(jnp.float32)
    width = N_FREQ / FX
    sub = lax.broadcasted_iota(jnp.int32, shape, 0).astype(jnp.float32)
    k1 = jnp.full(shape, -N_FREQ / 2.0 + (fx + 0.5) * width, jnp.float32)
    k2 = -N_FREQ / 2.0 + (fy0 + sub + 0.5) * width
    for level in range(LEVELS + 1):
        for path in range(2**level):
            off = path_offset(level, path)
            sq1[path_base(level) + path] = (k1 + off) * (k1 + off)
            sq2[path_base(level) + path] = (k2 + off) * (k2 + off)
    interp_rows(node_ref, w_ref)
    upper = row(6) > 0.5
    for level in range(LEVELS + 1):
        n = boxes_at(level)
        w = 1.0 / n
        across, down = max(n // 2, 1), max(n // 2, 1)
        part_x = [turn((sx + 0.5) * w + w * row(0)) for sx in range(across)]
        part_y = []
        for pair in range(down):
            center = (2 * pair + row(6) + 0.5) * w if level < LEVELS else 0.5
            part_y.append(turn(center + w * row(1)))
        for sx in range(across):
            for pair in range(down):
                c1 = (2.0 + part_x[sx][1] * part_y[pair][1]) / 16.0
                c2 = (2.0 + part_x[sx][0] * part_y[pair][0]) / 16.0
                at = point_base(level) + sx * down + pair
                pp[at] = c1 * c1
                qq[at] = c2 * c2

    def frac(v):
        return v - jnp.floor(v)

    w = 1.0 / BOXES
    for jx in range(2):
        for jy in range(2):
            s1 = w * (k1 + path_offset(1, jx))
            s2 = w * (k2 + path_offset(1, jy))
            along = frac(row(2) * s1) + row(3) * s1 + frac(row(4) * s2) + row(5) * s2
            lin[2 * jx + jy] = along
            lin[4 + 2 * jx + jy] = (N_FREQ / FX / 4) / BOXES * ((2 * jx - 1) * row(0) + (2 * jy - 1) * row(1))

    @pl.loop(0, 8)
    def _(sx):
        for pair in range(8):
            p, q = pp[sx * 8 + pair], qq[sx * 8 + pair]
            for jx in range(2):
                for jy in range(2):
                    r = jnp.sqrt(p * sq1[1 + jx] + q * sq2[1 + jy])
                    c, s = turn(r - jnp.round(r) + lin[2 * jx + jy])
                    at = (2 * jx + jy) * 64 + sx * 8 + pair
                    cos0_ref[at] = c
                    sin0_ref[at] = s

    def level_of(level, ax, ay, sx, pair):
        start = TABLE_BASE[level]
        n = boxes_at(level)
        half, span = n // 2, 2**level
        point = point_base(level) + sx * half + pair
        p, q = pp[point], qq[point]
        base = path_base(level)
        r0 = jnp.sqrt(p * sq1[base + ax] + q * sq2[base + ay])
        nxt = path_base(level + 1)
        for jx in range(2):
            for jy in range(2):
                j = 2 * jx + jy
                r = jnp.sqrt(p * sq1[nxt + ax + jx * span] + q * sq2[nxt + ay + jy * span])
                c, s = turn((r - r0) + lin[4 + j])
                path = j * span * span + ax * span + ay
                if level < 3:
                    at = start + (path * half + sx) * half + pair
                    cos_ref[at] = c
                    sin_ref[at] = s
                else:
                    at = start + 2 * path
                    cos_ref[at] = c
                    sin_ref[at] = s
                    cos_ref[at + 1] = pltpu.roll(c, POINTS, 1)
                    sin_ref[at + 1] = pltpu.roll(s, POINTS, 1)

    @pl.loop(0, 16)
    def _(step):
        a, sx = step // 4, step % 4
        for pair in range(4):
            level_of(1, a // 2, a % 2, sx, pair)

    flush(0)

    @pl.loop(0, 16)
    def _(a):
        for sx in range(2):
            for pair in range(2):
                level_of(2, a // 4, a % 4, sx, pair)

    flush(1)

    @pl.loop(0, 16)
    def _(step):
        for a in range(4):
            level_of(3, step // 2, step % 2 * 4 + a, 0, 0)

    flush(2)

    base = path_base(LEVELS)
    for pair in range(8):
        off = jnp.where(upper, path_offset(LEVELS, 2 * pair + 1), path_offset(LEVELS, 2 * pair))
        k = k2 + off
        sqp[pair] = k * k
        lin[8 + pair] = frac(row(4) * k) + row(5) * k
    for path in range(16):
        k = k1 + path_offset(LEVELS, path)
        lin[16 + path] = frac(row(2) * k) + row(3) * k

    @pl.loop(0, 16)
    def _(ax):
        p, q = pp[point_base(LEVELS)], qq[point_base(LEVELS)]
        for pair in range(8):
            r = jnp.sqrt(p * sq1[base + ax] + q * sqp[pair])
            c, s = turn(r - jnp.round(r) + lin[16 + ax] + lin[8 + pair])
            cos_ref[TABLE_BASE[LEVELS] + ax * 8 + pair] = c
            sin_ref[TABLE_BASE[LEVELS] + ax * 8 + pair] = s

    flush(3)
    for part in range(4):
        for copy in part_copies(send, part):
            copy.wait()


def merge_kernel(data_ref, w_ref, cos0_ref, sin0_ref, rest_ref, out_ref, ar, ai, br, bi, lhs_a, lhs_b, cos_rest, sin_rest, sems):
    def fetch(which, rows, sem):
        held = (cos_rest, sin_rest)[which]
        return pltpu.make_async_copy(rest_ref.at[which, rows], held.at[rows], sems.at[sem])

    for part in range(4):
        for copy in part_copies(fetch, part):
            copy.start()
    buffers = (None, (ar, ai), (br, bi), (ar, ai))
    w = w_ref[...]

    for level in range(LEVELS):
        n = boxes_at(level)
        half, span = n // 2, 2**level
        quarter = n // 4
        cos_ref, sin_ref = (cos_rest, sin_rest) if level else (cos0_ref, sin0_ref)
        if level:
            for part in (level - 1,) if level < 3 else (2, 3):
                for copy in part_copies(fetch, part):
                    copy.wait()
        count = (half * half if level < 3 else 2) * span * span

        def load(index, level=level):
            if level == 0:
                return data_ref[index, 0:ROWS], data_ref[index, ROWS : 2 * ROWS]
            return buffers[level][0][index], buffers[level][1][index]

        def source(q, cx, e, level=level, n=n, half=half, quarter=quarter):
            if level == 3:
                index = (2 * q + e) * 2 + cx
                return index, index
            m, pair = q // quarter, 2 * (q % quarter) + e
            a, sx = m // half, 2 * (m % half) + cx
            index = (a * n + sx) * half + pair
            if sx >= half:
                sx, pair = sx - half, (pair + quarter) % half
            return index, (a * half + sx) * half + pair

        def mix(j, part, lhs, load=load, source=source, base=TABLE_BASE[level], count=count,
                cos_ref=cos_ref, sin_ref=sin_ref):
            for i in range(0, 16, 2):
                for cx in range(2):
                    for e in range(2):
                        pieces = []
                        for q in (16 * part + i, 16 * part + i + 1):
                            index, factor = source(q, cx, e)
                            xr, xi = load(index)
                            at = base + j * count + factor
                            c, s = cos_ref[at], sin_ref[at]
                            pieces.append((xr * c - xi * s, xr * s + xi * c))
                        lanes = slice(LANES * (2 * cx + e), LANES * (2 * cx + e + 1))
                        for which in range(2):
                            value = jnp.concatenate([pieces[0][which], pieces[1][which]], axis=0)
                            high = value.astype(jnp.bfloat16)
                            low = (value - high.astype(jnp.float32)).astype(jnp.bfloat16)
                            at = 32 * i + 32 * which
                            lhs[at : at + 16, lanes] = high
                            lhs[at + 16 : at + 32, lanes] = low

        def store(j, part, lhs, level=level, n=n, span=span):
            jx, jy = j // 2, j % 2
            total = jnp.dot(lhs[...], w, preferred_element_type=jnp.float32)
            for i in range(16):
                q = 16 * part + i
                parts = []
                for which in range(2):
                    at = 32 * (i - i % 2) + 32 * which + 8 * (i % 2)
                    high, low = total[at : at + 8], total[at + 16 : at + 24]
                    parts.append(high[:, 0:LANES] + high[:, LANES:] + low[:, 0:LANES])
                re, im = parts
                if level < 3:
                    block = n * n // 8
                    a, rest = q // block, q % block
                    ax, ay = a // span, a % span
                    at = ((jx * span + ax) * 2 * span + jy * span + ay) * block + rest
                    buffers[level + 1][0][at] = re
                    buffers[level + 1][1][at] = im
                else:
                    ax, pair = q // 4, q % 4
                    at = (jx * 8 + ax) * 8 + jy * 4 + pair
                    c, s = cos_rest[TABLE_BASE[LEVELS] + at], sin_rest[TABLE_BASE[LEVELS] + at]
                    out_ref[at, 0:ROWS] = re * c + im * s
                    out_ref[at, ROWS : 2 * ROWS] = im * c - re * s

        @pl.loop(0, 4)
        def _(j, mix=mix, store=store):
            mix(j, 0, lhs_a)
            mix(j, 1, lhs_b)
            store(j, 0, lhs_a)
            store(j, 1, lhs_b)


def tables(owner):
    f32 = jnp.float32
    vreg = (ROWS, LANES)
    full = pl.BlockSpec(memory_space=pltpu.VMEM)
    return pl.pallas_call(
        table_kernel,
        out_shape=[jax.ShapeDtypeStruct((4 * LANES, 2 * LANES), jnp.bfloat16)]
        + [jax.ShapeDtypeStruct((256,) + vreg, f32)] * 2
        + [jax.ShapeDtypeStruct((2, TABLE_SIZE) + vreg, f32)],
        in_specs=[pl.BlockSpec(memory_space=pltpu.SMEM), full],
        out_specs=[full] * 3 + [pl.BlockSpec(memory_space=pltpu.MemorySpace.HBM)],
        scratch_shapes=[pltpu.VMEM((size,) + vreg, f32) for size in (31, 31, 8, 88, 88, 32, TABLE_SIZE, TABLE_SIZE)]
        + [pltpu.SemaphoreType.DMA((8,))],
        cost_estimate=pl.CostEstimate(flops=40_000_000, bytes_accessed=11 << 20, transcendentals=1_400_000),
        compiler_params=pltpu.CompilerParams(vmem_limit_bytes=50 << 20),
        name="phase_tables",
    )(owner, jnp.asarray(node_rows()))


def merge(data, weights, cosines, sines, rest):
    f32 = jnp.float32
    vreg = (ROWS, LANES)
    full = pl.BlockSpec(memory_space=pltpu.VMEM)
    return pl.pallas_call(
        merge_kernel,
        out_shape=jax.ShapeDtypeStruct((128, 2 * ROWS, LANES), f32),
        in_specs=[full] * 4 + [pl.BlockSpec(memory_space=pltpu.MemorySpace.HBM)],
        out_specs=full,
        scratch_shapes=[pltpu.VMEM((128,) + vreg, f32)] * 4 + [pltpu.VMEM((512, 512), jnp.bfloat16)] * 2
        + [pltpu.VMEM((TABLE_SIZE,) + vreg, f32)] * 2
        + [pltpu.SemaphoreType.DMA((8,))],
        cost_estimate=pl.CostEstimate(flops=2_000_000_000, bytes_accessed=13 << 20, transcendentals=0),
        compiler_params=pltpu.CompilerParams(vmem_limit_bytes=47 << 20),
        name="merge_levels",
    )(data, weights, cosines, sines, rest)


def on_device(weights_re, weights_im):
    devices = 128
    owner = lax.axis_index("bx") * lax.axis_size("by") + lax.axis_index("by")
    sent = jnp.concatenate(
        [weights_re.reshape(devices, ROWS, LANES), weights_im.reshape(devices, ROWS, LANES)], axis=1
    )
    data = lax.all_to_all(sent, ("bx", "by"), 0, 0, tiled=True)
    result = merge(data, *tables(owner.astype(jnp.int32).reshape(1)))
    back = lax.all_to_all(result, ("bx", "by"), 0, 0, tiled=True)
    shape = (devices * ROWS, 1, LANES)
    return back[:, :ROWS].reshape(shape), back[:, ROWS:].reshape(shape)


def solution(mesh):
    specs = (P(None, "bx", "by"), P(None, "bx", "by"))
    return jax.shard_map(on_device, mesh=mesh, in_specs=specs, out_specs=specs, check_vma=False)
```

time: 84.5 us -> 65.4 us (0.77)
  local copies, waits for them, and re-layouts: 21.8 us -> 1.72 us
  waiting for transfers between devices: 0.01 us -> 7.75 us
  blocking collectives: 28.6 us -> 23.2 us
  other arithmetic: 3.13 us -> 2.22 us
    unnamed x44 -> x2, local copies, waits for them, and re-layouts: 20 us -> 0.68 us
    all_to_all x1, waiting for transfers between devices: 0.01 us -> 7.75 us  [on_device(): data = lax.all_to_all(sent, ('bx', 'by'), 0, 0, tiled=True)]
    all_to_all x1, blocking collectives: 28.6 us -> 23.2 us  [on_device(): back = lax.all_to_all(result, ('bx', 'by'), 0, 0, tiled=True)]
    pallas_call x1, Pallas kernels: 9.51 us -> 7.71 us  [merge(): pl.pallas_call(merge_kernel, out_shape=jax.ShapeDtypeStruct((128, 2 * ROW...]
    pallas_call x1, Pallas kernels: 8.83 us -> 10.6 us  [tables(): pl.pallas_call(table_kernel, out_shape=[jax.ShapeDtypeStruct((4 * LANES,...]
  transfers between devices with their start and end apart: 1 -> 1, of which waited for: 0 -> 1; matrix products, arithmetic and copies ran while one was open for 2% -> 0% of each run, Pallas kernels for 11% -> 16%
where the time goes in v2:
time: 65.4 us; the launch traced here: 65.1 us
  blocking collectives  23.2 us (35%)
  Pallas kernels  18.3 us (28%)
  starting transfers between devices  11.2 us (17%)
  waiting for transfers between devices  7.75 us (12%)
  other arithmetic  2.22 us (3%)
  local copies, waits for them, and re-layouts  1.72 us (3%)
  between operations  0.67 us (1%)
    all_to_all x1, blocking collectives, on_device(): back = lax.all_to_all(result, ('bx', 'by'), 0, 0, tiled=True)  23.2 us
    all_to_all x1, starting transfers between devices, on_device(): data = lax.all_to_all(sent, ('bx', 'by'), 0, 0, tiled=True)  11.2 us
    pallas_call x1, Pallas kernels, tables(): pl.pallas_call(table_kernel, out_shape=[jax.ShapeDtypeStruct((4 * LANES,...  10.6 us
    all_to_all x1, waiting for transfers between devices, on_device(): data = lax.all_to_all(sent, ('bx', 'by'), 0, 0, tiled=True)  7.75 us
    pallas_call x1, Pallas kernels, merge(): pl.pallas_call(merge_kernel, out_shape=jax.ShapeDtypeStruct((128, 2 * ROW...  7.71 us
    concatenate x1, other arithmetic, on_device(): jnp.concatenate([weights_re.reshape(devices, ROWS, LANES), weights_im.res...  2.22 us
  transfers between devices with their start and end apart: 1, of which 1 were waited for; matrix products, arithmetic and copies ran while one was open for 0% of the time, Pallas kernels for 16%

profile of v2, /device:TPU:0, one launch (start us, length us, event | category | flops | bytes accessed | tf_op | source)
XLA Modules:
  0.0 65.1 jit_solution(3877035730972956638)
XLA Ops:
  0.6 2.2 %pad_maximum_fusion = f32[128,16,128]{2,1,0:T(8,128)} fusion(f32[128,8,128]{2,1,0:T(8,128)} %bitcast.9, f32[128,8,128]{2,1,0:T(8,128)} %bitcast.10), kind=kLoop, calls=%fused_computation | loop fusion | flops 262144 | bytes 2097152 | tf_op jit(solution)/shard_map/concatenate | solution.py:391
  2.8 11.2 %all-to-all-start = ((f32[128,16,128]{2,1,0:T(8,128)}), f32[128,16,128]{2,1,0:T(8,128)S(1)}, u32[]{:S(2)}, u32[]{:S(2)}) async-start(f32[128,16,128]{2,1,0:T(8,128)} %pad_maximum_fusion), calls=%async_computation | async-start | bytes 2097152 | tf_op jit(solution)/shard_map/all_to_all | solution.py:394
  14.0 0.0 copy-start
  14.0 0.7 %copy-done = f32[8,128]{1,0:T(8,128)S(1)} copy-done((f32[8,128]{1,0:T(8,128)S(1)}, f32[8,128]{1,0:T(8,128)}, u32[]{:S(2)}) %copy-start) | copy-done | bytes 4120
  14.7 10.6 %phase_tables.1 = (bf16[512,256]{1,0:T(8,128)(2,1)S(1)}, f32[256,8,128]{2,1,0:T(8,128)S(1)}, f32[256,8,128]{2,1,0:T(8,128)S(1)}, f32[2,1152,8,128]{3,2,1,0:T(8,128)}) custom-call(s32[1]{0:T(128)} %bitcast.2.owner_ref, f32[8,128]{1,0:T(8,128)S(1)} %copy-done), custom_call_target="tpu_custom_call" | custom-call | flops 40000000 | bytes 11534336 | tf_op jit(solution)/shard_map/phase_tables/pallas_call | solution.py:355
  25.3 7.8 %all-to-all-done.data_ref = f32[128,16,128]{2,1,0:T(8,128)S(1)} async-done(((f32[128,16,128]{2,1,0:T(8,128)}), f32[128,16,128]{2,1,0:T(8,128)S(1)}, u32[]{:S(2)}, u32[]{:S(2)}) %all-to-all-start) | async-done | bytes 1048608 | tf_op jit(solution)/shard_map/all_to_all | solution.py:394
  33.1 7.7 %merge_levels.1 = f32[128,16,128]{2,1,0:T(8,128)S(1)} custom-call(f32[128,16,128]{2,1,0:T(8,128)S(1)} %all-to-all-done.data_ref, bf16[512,256]{1,0:T(8,128)(2,1)S(1)} %get-tuple-element.6.w_ref, f32[256,8,128]{2,1,0:T(8,128)S(1)} %get-tuple-element.7.cos0_ref, f32[256,8,128]{2,1,0:T(8,128)S(1)} %get-tuple-element.8.sin0_ref, ...), custom_call_target="tpu_custom_call" | custom-call | flops 2000000000 | bytes 13631488 | tf_op jit(solution)/shard_map/merge_levels/pallas_call | solution.py:374
  40.8 23.2 %all_to_all.10 = f32[128,16,128]{2,1,0:T(8,128)S(1)} all-to-all(f32[128,16,128]{2,1,0:T(8,128)S(1)} %merge_levels.1), channel_id=1, replica_groups=mesh['bx'=16,'by'=8] {'bx','by'}, dimensions={0} | all-to-all | bytes 2097152 | tf_op jit(solution)/shard_map/all_to_all | solution.py:396
  64.1 1.0 %fusion = (f32[128,8,128]{2,1,0:T(8,128)}, f32[128,8,128]{2,1,0:T(8,128)}) fusion(f32[128,16,128]{2,1,0:T(8,128)S(1)} %all_to_all.10), kind=kLoop, calls=%fused_computation.1 | loop fusion | bytes 2097152 | tf_op jit(solution)/shard_map/slice | solution.py:398
Async XLA Ops:
  2.8 30.2 %all-to-all-start = ((f32[128,16,128]{2,1,0:T(8,128)}), f32[128,16,128]{2,1,0:T(8,128)S(1)}, u32[]{:S(2)}, u32[]{:S(2)}) async-start(f32[128,16,128]{2,1,0:T(8,128)} %pad_maximum_fusion), calls=%async_computation | async-start | bytes 2097152 | tf_op jit(solution)/shard_map/all_to_all | solution.py:394
  14.0 0.7 %copy-start = (f32[8,128]{1,0:T(8,128)S(1)}, f32[8,128]{1,0:T(8,128)}, u32[]{:S(2)}) copy-start(f32[8,128]{1,0:T(8,128)} %constant.13.clone.node_ref) | copy-start | bytes 12292

commit v3 on v2

--- a/solution.py
+++ b/solution.py
@@ -256,7 +256,7 @@
             copy.wait()
 
 
-def merge_kernel(data_ref, w_ref, cos0_ref, sin0_ref, rest_ref, out_ref, ar, ai, br, bi, lhs_a, lhs_b, cos_rest, sin_rest, sems):
+def merge_kernel(data_ref, w_ref, cos0_ref, sin0_ref, rest_ref, out_ref, ar, ai, br, bi, lhs_a, lhs_b, lhs_c, lhs_d, cos_rest, sin_rest, sems):
     def fetch(which, rows, sem):
         held = (cos_rest, sin_rest)[which]
         return pltpu.make_async_copy(rest_ref.at[which, rows], held.at[rows], sems.at[sem])
@@ -265,8 +265,6 @@
         for copy in part_copies(fetch, part):
             copy.start()
     buffers = (None, (ar, ai), (br, bi), (ar, ai))
-    w = w_ref[...]
-
     for level in range(LEVELS):
         n = boxes_at(level)
         half, span = n // 2, 2**level
@@ -306,18 +304,19 @@
                             at = base + j * count + factor
                             c, s = cos_ref[at], sin_ref[at]
                             pieces.append((xr * c - xi * s, xr * s + xi * c))
-                        lanes = slice(LANES * (2 * cx + e), LANES * (2 * cx + e + 1))
+                        k = 2 * cx + e
                         for which in range(2):
                             value = jnp.concatenate([pieces[0][which], pieces[1][which]], axis=0)
                             high = value.astype(jnp.bfloat16)
                             low = (value - high.astype(jnp.float32)).astype(jnp.bfloat16)
                             at = 32 * i + 32 * which
-                            lhs[at : at + 16, lanes] = high
-                            lhs[at + 16 : at + 32, lanes] = low
+                            lhs[k, at : at + 16] = high
+                            lhs[k, at + 16 : at + 32] = low
 
         def store(j, part, lhs, level=level, n=n, span=span):
             jx, jy = j // 2, j % 2
-            total = jnp.dot(lhs[...], w, preferred_element_type=jnp.float32)
+            rows = jnp.concatenate([lhs[k] for k in range(4)], axis=1)
+            total = jnp.dot(rows, w_ref[...], preferred_element_type=jnp.float32)
             for i in range(16):
                 q = 16 * part + i
                 parts = []
@@ -340,12 +339,16 @@
                     out_ref[at, 0:ROWS] = re * c + im * s
                     out_ref[at, ROWS : 2 * ROWS] = im * c - re * s
 
-        @pl.loop(0, 4)
-        def _(j, mix=mix, store=store):
-            mix(j, 0, lhs_a)
-            mix(j, 1, lhs_b)
-            store(j, 0, lhs_a)
-            store(j, 1, lhs_b)
+        @pl.loop(0, 2)
+        def _(jx, mix=mix, store=store):
+            mix(2 * jx, 0, lhs_a)
+            mix(2 * jx, 1, lhs_b)
+            store(2 * jx, 0, lhs_a)
+            mix(2 * jx + 1, 0, lhs_c)
+            store(2 * jx, 1, lhs_b)
+            mix(2 * jx + 1, 1, lhs_d)
+            store(2 * jx + 1, 0, lhs_c)
+            store(2 * jx + 1, 1, lhs_d)
 
 
 def tables(owner):
@@ -376,7 +379,7 @@
         out_shape=jax.ShapeDtypeStruct((128, 2 * ROWS, LANES), f32),
         in_specs=[full] * 4 + [pl.BlockSpec(memory_space=pltpu.MemorySpace.HBM)],
         out_specs=full,
-        scratch_shapes=[pltpu.VMEM((128,) + vreg, f32)] * 4 + [pltpu.VMEM((512, 512), jnp.bfloat16)] * 2
+        scratch_shapes=[pltpu.VMEM((128,) + vreg, f32)] * 4 + [pltpu.VMEM((4, 512, LANES), jnp.bfloat16)] * 4
         + [pltpu.VMEM((TABLE_SIZE,) + vreg, f32)] * 2
         + [pltpu.SemaphoreType.DMA((8,))],
         cost_estimate=pl.CostEstimate(flops=2_000_000_000, bytes_accessed=13 << 20, transcendentals=0),

time: 65.4 us -> 63.8 us (0.976)
  Pallas kernels: 18.3 us -> 16.7 us
    pallas_call x1, Pallas kernels: 7.71 us -> 6.13 us  [merge(): pl.pallas_call(merge_kernel, out_shape=jax.ShapeDtypeStruct((128, 2 * ROW...]
  transfers between devices with their start and end apart: 1 -> 1, of which waited for: 1 -> 1; matrix products, arithmetic and copies ran while one was open for 0% -> 0% of each run, Pallas kernels for 16% -> 17%
where the time goes in v3:
time: 63.8 us; the launch traced here: 63.5 us
  blocking collectives  23.3 us (37%)
  Pallas kernels  16.7 us (26%)
  starting transfers between devices  11.2 us (18%)
  waiting for transfers between devices  7.75 us (12%)
  other arithmetic  2.22 us (3%)
  local copies, waits for them, and re-layouts  1.72 us (3%)
  between operations  0.67 us (1%)
    all_to_all x1, blocking collectives, on_device(): back = lax.all_to_all(result, ('bx', 'by'), 0, 0, tiled=True)  23.3 us
    all_to_all x1, starting transfers between devices, on_device(): data = lax.all_to_all(sent, ('bx', 'by'), 0, 0, tiled=True)  11.2 us
    pallas_call x1, Pallas kernels, tables(): pl.pallas_call(table_kernel, out_shape=[jax.ShapeDtypeStruct((4 * LANES,...  10.6 us
    all_to_all x1, waiting for transfers between devices, on_device(): data = lax.all_to_all(sent, ('bx', 'by'), 0, 0, tiled=True)  7.75 us
    pallas_call x1, Pallas kernels, merge(): pl.pallas_call(merge_kernel, out_shape=jax.ShapeDtypeStruct((128, 2 * ROW...  6.13 us
    concatenate x1, other arithmetic, on_device(): jnp.concatenate([weights_re.reshape(devices, ROWS, LANES), weights_im.res...  2.22 us
  transfers between devices with their start and end apart: 1, of which 1 were waited for; matrix products, arithmetic and copies ran while one was open for 0% of the time, Pallas kernels for 17%

profile of v3, /device:TPU:0, one launch (start us, length us, event | category | flops | bytes accessed | tf_op | source)
XLA Modules:
  0.0 63.5 jit_solution(5121453172962357544)
XLA Ops:
  0.6 2.2 %pad_maximum_fusion = f32[128,16,128]{2,1,0:T(8,128)} fusion(f32[128,8,128]{2,1,0:T(8,128)} %bitcast.9, f32[128,8,128]{2,1,0:T(8,128)} %bitcast.10), kind=kLoop, calls=%fused_computation | loop fusion | flops 262144 | bytes 2097152 | tf_op jit(solution)/shard_map/concatenate | solution.py:394
  2.8 11.2 %all-to-all-start = ((f32[128,16,128]{2,1,0:T(8,128)}), f32[128,16,128]{2,1,0:T(8,128)S(1)}, u32[]{:S(2)}, u32[]{:S(2)}) async-start(f32[128,16,128]{2,1,0:T(8,128)} %pad_maximum_fusion), calls=%async_computation | async-start | bytes 2097152 | tf_op jit(solution)/shard_map/all_to_all | solution.py:397
  14.0 0.0 copy-start
  14.0 0.7 %copy-done = f32[8,128]{1,0:T(8,128)S(1)} copy-done((f32[8,128]{1,0:T(8,128)S(1)}, f32[8,128]{1,0:T(8,128)}, u32[]{:S(2)}) %copy-start) | copy-done | bytes 4120
  14.7 10.6 %phase_tables.1 = (bf16[512,256]{1,0:T(8,128)(2,1)S(1)}, f32[256,8,128]{2,1,0:T(8,128)S(1)}, f32[256,8,128]{2,1,0:T(8,128)S(1)}, f32[2,1152,8,128]{3,2,1,0:T(8,128)}) custom-call(s32[1]{0:T(128)} %bitcast.2.owner_ref, f32[8,128]{1,0:T(8,128)S(1)} %copy-done), custom_call_target="tpu_custom_call" | custom-call | flops 40000000 | bytes 11534336 | tf_op jit(solution)/shard_map/phase_tables/pallas_call | solution.py:358
  25.3 7.8 %all-to-all-done.data_ref = f32[128,16,128]{2,1,0:T(8,128)S(1)} async-done(((f32[128,16,128]{2,1,0:T(8,128)}), f32[128,16,128]{2,1,0:T(8,128)S(1)}, u32[]{:S(2)}, u32[]{:S(2)}) %all-to-all-start) | async-done | bytes 1048608 | tf_op jit(solution)/shard_map/all_to_all | solution.py:397
  33.1 6.1 %merge_levels.1 = f32[128,16,128]{2,1,0:T(8,128)S(1)} custom-call(f32[128,16,128]{2,1,0:T(8,128)S(1)} %all-to-all-done.data_ref, bf16[512,256]{1,0:T(8,128)(2,1)S(1)} %get-tuple-element.6.w_ref, f32[256,8,128]{2,1,0:T(8,128)S(1)} %get-tuple-element.7.cos0_ref, f32[256,8,128]{2,1,0:T(8,128)S(1)} %get-tuple-element.8.sin0_ref, ...), custom_call_target="tpu_custom_call" | custom-call | flops 2000000000 | bytes 13631488 | tf_op jit(solution)/shard_map/merge_levels/pallas_call | solution.py:377
  39.2 23.3 %all_to_all.10 = f32[128,16,128]{2,1,0:T(8,128)S(1)} all-to-all(f32[128,16,128]{2,1,0:T(8,128)S(1)} %merge_levels.1), channel_id=1, replica_groups=mesh['bx'=16,'by'=8] {'bx','by'}, dimensions={0} | all-to-all | bytes 2097152 | tf_op jit(solution)/shard_map/all_to_all | solution.py:399
  62.5 1.0 %fusion = (f32[128,8,128]{2,1,0:T(8,128)}, f32[128,8,128]{2,1,0:T(8,128)}) fusion(f32[128,16,128]{2,1,0:T(8,128)S(1)} %all_to_all.10), kind=kLoop, calls=%fused_computation.1 | loop fusion | bytes 2097152 | tf_op jit(solution)/shard_map/slice | solution.py:401
Async XLA Ops:
  2.8 30.2 %all-to-all-start = ((f32[128,16,128]{2,1,0:T(8,128)}), f32[128,16,128]{2,1,0:T(8,128)S(1)}, u32[]{:S(2)}, u32[]{:S(2)}) async-start(f32[128,16,128]{2,1,0:T(8,128)} %pad_maximum_fusion), calls=%async_computation | async-start | bytes 2097152 | tf_op jit(solution)/shard_map/all_to_all | solution.py:397
  14.0 0.7 %copy-start = (f32[8,128]{1,0:T(8,128)S(1)}, f32[8,128]{1,0:T(8,128)}, u32[]{:S(2)}) copy-start(f32[8,128]{1,0:T(8,128)} %constant.13.clone.node_ref) | copy-start | bytes 12292

commit v4 on v3

--- a/solution.py
+++ b/solution.py
@@ -74,6 +74,7 @@
 
 TABLE_BASE = (0, 0, 256, 512, 1024)
 TABLE_SIZE = 1152
+STACK_PARTS = 2
 TABLE_PARTS = ((0, 256), (256, 256), (512, 512), (1024, 128))
 
 
@@ -388,11 +389,54 @@
     )(data, weights, cosines, sines, rest)
 
 
+def stack_kernel(re_ref, im_ref, out_ref, held, in_sems, out_sems):
+    size = 128 // STACK_PARTS
+
+    def inward(part, which):
+        rows = pl.ds(part * size, size)
+        source = (re_ref, im_ref)[which]
+        return pltpu.make_async_copy(
+            source.at[rows], held.at[rows, pl.ds(which * ROWS, ROWS)], in_sems.at[2 * part + which]
+        )
+
+    def outward(part):
+        rows = pl.ds(part * size, size)
+        return pltpu.make_async_copy(held.at[rows], out_ref.at[rows], out_sems.at[part])
+
+    for part in range(STACK_PARTS):
+        for which in range(2):
+            inward(part, which).start()
+    for part in range(STACK_PARTS):
+        for which in range(2):
+            inward(part, which).wait()
+        outward(part).start()
+    for part in range(STACK_PARTS):
+        outward(part).wait()
+
+
+def stacked(first, second):
+    anywhere = pl.BlockSpec(memory_space=pl.ANY)
+    return pl.pallas_call(
+        stack_kernel,
+        out_shape=jax.ShapeDtypeStruct((128, 2 * ROWS, LANES), jnp.float32),
+        in_specs=[anywhere] * 2,
+        out_specs=anywhere,
+        scratch_shapes=[
+            pltpu.VMEM((128, 2 * ROWS, LANES), jnp.float32),
+            pltpu.SemaphoreType.DMA((2 * STACK_PARTS,)),
+            pltpu.SemaphoreType.DMA((STACK_PARTS,)),
+        ],
+        cost_estimate=pl.CostEstimate(flops=0, bytes_accessed=2 << 20, transcendentals=0),
+        compiler_params=pltpu.CompilerParams(vmem_limit_bytes=58 << 20),
+        name="stack_parts",
+    )(first, second)
+
+
 def on_device(weights_re, weights_im):
     devices = 128
     owner = lax.axis_index("bx") * lax.axis_size("by") + lax.axis_index("by")
-    sent = jnp.concatenate(
-        [weights_re.reshape(devices, ROWS, LANES), weights_im.reshape(devices, ROWS, LANES)], axis=1
+    sent = stacked(
+        weights_re.reshape(devices, ROWS, LANES), weights_im.reshape(devices, ROWS, LANES)
     )
     data = lax.all_to_all(sent, ("bx", "by"), 0, 0, tiled=True)
     result = merge(data, *tables(owner.astype(jnp.int32).reshape(1)))

time: 63.8 us -> 63.6 us (level)
  other arithmetic: 2.22 us -> 0 us
  Pallas kernels: 16.7 us -> 18.8 us
    concatenate x1 -> x0, other arithmetic: 2.22 us -> none  [on_device(): jnp.concatenate([weights_re.reshape(devices, ROWS, LANES), weights_im.res...]
    pallas_call x0 -> x1, Pallas kernels: none -> 2.03 us  [stacked(): pl.pallas_call(stack_kernel, out_shape=jax.ShapeDtypeStruct((128, 2 * ROW...]
where the time goes in v4:
time: 63.6 us; the launch traced here: 63.4 us
  blocking collectives  23.3 us (37%)
  Pallas kernels  18.8 us (30%)
  starting transfers between devices  11.2 us (18%)
  waiting for transfers between devices  7.75 us (12%)
  local copies, waits for them, and re-layouts  1.72 us (3%)
  between operations  0.68 us (1%)
    all_to_all x1, blocking collectives, on_device(): back = lax.all_to_all(result, ('bx', 'by'), 0, 0, tiled=True)  23.3 us
    all_to_all x1, starting transfers between devices, on_device(): data = lax.all_to_all(sent, ('bx', 'by'), 0, 0, tiled=True)  11.2 us
    pallas_call x1, Pallas kernels, tables(): pl.pallas_call(table_kernel, out_shape=[jax.ShapeDtypeStruct((4 * LANES,...  10.6 us
    all_to_all x1, waiting for transfers between devices, on_device(): data = lax.all_to_all(sent, ('bx', 'by'), 0, 0, tiled=True)  7.75 us
    pallas_call x1, Pallas kernels, merge(): pl.pallas_call(merge_kernel, out_shape=jax.ShapeDtypeStruct((128, 2 * ROW...  6.12 us
    pallas_call x1, Pallas kernels, stacked(): pl.pallas_call(stack_kernel, out_shape=jax.ShapeDtypeStruct((128, 2 * ROW...  2.03 us
  transfers between devices with their start and end apart: 1, of which 1 were waited for; matrix products, arithmetic and copies ran while one was open for 0% of the time, Pallas kernels for 17%

profile of v4, /device:TPU:0, one launch (start us, length us, event | category | flops | bytes accessed | tf_op | source)
XLA Modules:
  0.0 63.4 jit_solution(11931800689373716280)
XLA Ops:
  0.6 2.0 %stack_parts.1 = f32[128,16,128]{2,1,0:T(8,128)} custom-call(f32[128,8,128]{2,1,0:T(8,128)} %bitcast.9, f32[128,8,128]{2,1,0:T(8,128)} %bitcast.10), custom_call_target="tpu_custom_call" | custom-call | bytes 2097152 | tf_op jit(solution)/shard_map/stack_parts/pallas_call | solution.py:419
  2.7 11.2 %all-to-all-start = ((f32[128,16,128]{2,1,0:T(8,128)}), f32[128,16,128]{2,1,0:T(8,128)S(1)}, u32[]{:S(2)}, u32[]{:S(2)}) async-start(f32[128,16,128]{2,1,0:T(8,128)} %stack_parts.1), calls=%async_computation | async-start | bytes 2097152 | tf_op jit(solution)/shard_map/all_to_all | solution.py:441
  13.9 0.0 copy-start
  13.9 0.7 %copy-done = f32[8,128]{1,0:T(8,128)S(1)} copy-done((f32[8,128]{1,0:T(8,128)S(1)}, f32[8,128]{1,0:T(8,128)}, u32[]{:S(2)}) %copy-start) | copy-done | bytes 4120
  14.6 10.6 %phase_tables.1 = (bf16[512,256]{1,0:T(8,128)(2,1)S(1)}, f32[256,8,128]{2,1,0:T(8,128)S(1)}, f32[256,8,128]{2,1,0:T(8,128)S(1)}, f32[2,1152,8,128]{3,2,1,0:T(8,128)}) custom-call(s32[1]{0:T(128)} %bitcast.2.owner_ref, f32[8,128]{1,0:T(8,128)S(1)} %copy-done), custom_call_target="tpu_custom_call" | custom-call | flops 40000000 | bytes 11534336 | tf_op jit(solution)/shard_map/phase_tables/pallas_call | solution.py:359
  25.2 7.8 %all-to-all-done.data_ref = f32[128,16,128]{2,1,0:T(8,128)S(1)} async-done(((f32[128,16,128]{2,1,0:T(8,128)}), f32[128,16,128]{2,1,0:T(8,128)S(1)}, u32[]{:S(2)}, u32[]{:S(2)}) %all-to-all-start) | async-done | bytes 1048608 | tf_op jit(solution)/shard_map/all_to_all | solution.py:441
  32.9 6.1 %merge_levels.1 = f32[128,16,128]{2,1,0:T(8,128)S(1)} custom-call(f32[128,16,128]{2,1,0:T(8,128)S(1)} %all-to-all-done.data_ref, bf16[512,256]{1,0:T(8,128)(2,1)S(1)} %get-tuple-element.6.w_ref, f32[256,8,128]{2,1,0:T(8,128)S(1)} %get-tuple-element.7.cos0_ref, f32[256,8,128]{2,1,0:T(8,128)S(1)} %get-tuple-element.8.sin0_ref, ...), custom_call_target="tpu_custom_call" | custom-call | flops 2000000000 | bytes 13631488 | tf_op jit(solution)/shard_map/merge_levels/pallas_call | solution.py:378
  39.0 23.3 %all_to_all.10 = f32[128,16,128]{2,1,0:T(8,128)S(1)} all-to-all(f32[128,16,128]{2,1,0:T(8,128)S(1)} %merge_levels.1), channel_id=1, replica_groups=mesh['bx'=16,'by'=8] {'bx','by'}, dimensions={0} | all-to-all | bytes 2097152 | tf_op jit(solution)/shard_map/all_to_all | solution.py:443
  62.3 1.0 %fusion = (f32[128,8,128]{2,1,0:T(8,128)}, f32[128,8,128]{2,1,0:T(8,128)}) fusion(f32[128,16,128]{2,1,0:T(8,128)S(1)} %all_to_all.10), kind=kLoop, calls=%fused_computation | loop fusion | bytes 2097152 | tf_op jit(solution)/shard_map/slice | solution.py:445
Async XLA Ops:
  2.7 30.2 %all-to-all-start = ((f32[128,16,128]{2,1,0:T(8,128)}), f32[128,16,128]{2,1,0:T(8,128)S(1)}, u32[]{:S(2)}, u32[]{:S(2)}) async-start(f32[128,16,128]{2,1,0:T(8,128)} %stack_parts.1), calls=%async_computation | async-start | bytes 2097152 | tf_op jit(solution)/shard_map/all_to_all | solution.py:441
  13.9 0.7 %copy-start = (f32[8,128]{1,0:T(8,128)S(1)}, f32[8,128]{1,0:T(8,128)}, u32[]{:S(2)}) copy-start(f32[8,128]{1,0:T(8,128)} %constant.13.clone.node_ref) | copy-start | bytes 12292
